TPU v7x, 256 devices: a whole 4x4x8 slice. The times are simulated.
256 devices in a mesh: seq: 32 (over y_lo, z, core), tp: 4 (over x), dp: 2 (over y_hi).
Axes of the slice: x: 4, y: 4 (y_hi: 2, y_lo: 2; y = y_hi * 2 + y_lo), z: 8, core: 2. Of those that a mesh axis runs over, the one named last changes fastest.
Arguments:
- query_gate: bfloat16 [2, 8192, 4096], P('dp', 'seq', 'tp'), may hold values from -6 to 6
- key_gate: bfloat16 [2, 8192, 4096], P('dp', 'seq', 'tp'), may hold values from -6 to 6
- value_input: bfloat16 [2, 8192, 4096], P('dp', 'seq', 'tp'), may hold values from -6 to 6
- filter_taps: bfloat16 [4096, 128], P('tp'), may hold values from -0.5 to 0.5
- skip_gain: float32 [4096], P('tp'), may hold values from -1 to 1
- out_weight: bfloat16 [4096, 4096], P('tp', 'dp'), may hold values from -0.09375 to 0.09375
- cotangent: bfloat16 [2, 8192, 4096], P('dp', 'seq', 'tp'), may hold values from -6 to 6
Outputs:
- grad_query: bfloat16 [2, 8192, 4096], P('dp', 'seq', 'tp')
- grad_key: bfloat16 [2, 8192, 4096], P('dp', 'seq', 'tp')
- grad_value: bfloat16 [2, 8192, 4096], P('dp', 'seq', 'tp')
- grad_filter: float32 [4096, 128], P('tp')
- grad_skip: float32 [4096], P('tp')
- grad_weight: float32 [4096, 4096], P(('seq', 'dp'), 'tp')
All inputs are finite; a program needn't handle non-finite values.
Results may differ from a plain program's by a relative error of at most 0.0095.
Values may be sent and summed in bfloat16 or wider, within the bound.
A program may use at most 192 MiB of HBM per device.

v0:
```python
import math

import jax
import jax.numpy as jnp
from jax import lax
from jax.sharding import PartitionSpec as P

block_rows = 16


def shifted(block, axis, distance):
    devices = range(lax.axis_size(axis))
    route = [(i - distance, i) for i in devices if i - distance in devices]
    return lax.ppermute(block, axis, route)


def taps_matrix(vector, row_count, col_count):
    channels, width_all = vector.shape
    tiled = jnp.tile(vector, (1, row_count + 1))
    skewed = tiled[:, : row_count * (width_all - 1)].reshape(channels, row_count, width_all - 1)
    return skewed[:, :, row_count - 1 : row_count - 1 + col_count]


def forward_table(filter_taps):
    channels, tap_count = filter_taps.shape
    padding = jnp.zeros((channels, block_rows), filter_taps.dtype)
    vector = jnp.concatenate([padding, filter_taps[:, ::-1], padding], axis=1)
    return taps_matrix(vector, block_rows, tap_count + block_rows)


def backward_table(filter_taps):
    channels, tap_count = filter_taps.shape
    before = jnp.zeros((channels, block_rows - 1), filter_taps.dtype)
    after = jnp.zeros((channels, block_rows + 1), filter_taps.dtype)
    vector = jnp.concatenate([before, filter_taps, after], axis=1)
    return taps_matrix(vector, block_rows, tap_count + block_rows)


def windows(extended, length, tap_count):
    pieces = []
    for shift_index in range(tap_count // block_rows + 1):
        lower = shift_index * block_rows
        pieces.append(
            extended[lower : lower + length].reshape(
                length // block_rows, block_rows, extended.shape[1]
            )
        )
    return jnp.concatenate(pieces, axis=1)


def lag_sums(blocks, tap_count):
    channels, row_count, col_count = blocks.shape
    flattened = blocks.reshape(channels, row_count * col_count)
    padded = jnp.concatenate([flattened, jnp.zeros((channels, row_count), blocks.dtype)], axis=1)
    diagonal = padded.reshape(channels, row_count, col_count + 1)[:, :, 1 : tap_count + 1]
    return jnp.sum(diagonal, axis=1)[:, ::-1]


def per_device(query_gate, key_gate, value_input, filter_taps, skip_gain, out_weight, cotangent):
    queries = query_gate[0]
    key_rows = key_gate[0]
    value_rows = value_input[0]
    length, channels = queries.shape
    tap_count = filter_taps.shape[1]
    seq_count = lax.axis_size("seq")
    replica_count = lax.axis_size("dp")
    norm_factor = 1.0 / math.sqrt(length * seq_count * replica_count)
    mixed = (key_rows.astype(jnp.float32) * value_rows.astype(jnp.float32)).astype(jnp.bfloat16)
    tail_rows = mixed[length - (tap_count - 1) :]
    prior = shifted(tail_rows, "seq", 1)
    extended = jnp.concatenate([jnp.zeros((1, channels), jnp.bfloat16), prior, mixed], axis=0)
    forward_windows = windows(extended, length, tap_count)
    conv = jnp.einsum(
        "cab,ibc->iac",
        forward_table(filter_taps),
        forward_windows,
        preferred_element_type=jnp.float32,
    ).reshape(length, channels)
    state = conv + skip_gain[None, :] * mixed.astype(jnp.float32)
    gated = (queries.astype(jnp.float32) * state).astype(jnp.bfloat16)
    full_cot = lax.all_gather(cotangent[0], "tp", axis=1, tiled=True)
    selected = full_cot
    grad_gated = lax.dot_general(
        selected,
        lax.all_gather(out_weight, "dp", axis=1, tiled=True),
        (((1,), (1,)), ((), ())),
        preferred_element_type=jnp.float32,
    )
    grad_query = (grad_gated * state).astype(jnp.bfloat16)
    signal = (grad_gated * queries.astype(jnp.float32)).astype(jnp.bfloat16)
    head_rows = signal[: tap_count - 1]
    later = shifted(head_rows, "seq", -1)
    signal_ext = jnp.concatenate([signal, later, jnp.zeros((1, channels), jnp.bfloat16)], axis=0)
    back = jnp.einsum(
        "cab,ibc->iac",
        backward_table(filter_taps),
        windows(signal_ext, length, tap_count),
        preferred_element_type=jnp.float32,
    ).reshape(length, channels)
    back = back + skip_gain[None, :] * signal.astype(jnp.float32)
    grad_key = (back * value_rows.astype(jnp.float32)).astype(jnp.bfloat16)
    grad_value = (back * key_rows.astype(jnp.float32)).astype(jnp.bfloat16)
    signal_blocks = signal.reshape(length // block_rows, block_rows, channels)
    blocks = jnp.einsum(
        "iac,ibc->cab", signal_blocks, forward_windows, preferred_element_type=jnp.float32
    )
    skip_term = jnp.sum(signal.astype(jnp.float32) * mixed.astype(jnp.float32), axis=0)
    filter_sum, skip_sum = lax.psum((lag_sums(blocks, tap_count), skip_term), ("seq", "dp"))
    selected = full_cot
    grad_weight = lax.psum_scatter(
        lax.dot_general(
            selected, gated, (((0,), (0,)), ((), ())), preferred_element_type=jnp.float32
        ),
        ("seq", "dp"),
        scatter_dimension=0,
        tiled=True,
    )
    return (
        grad_query[None],
        grad_key[None],
        grad_value[None],
        filter_sum * norm_factor,
        skip_sum * norm_factor,
        grad_weight * norm_factor,
    )


def solution(mesh):
    return jax.shard_map(
        per_device,
        mesh=mesh,
        in_specs=(
            P("dp", "seq", "tp"),
            P("dp", "seq", "tp"),
            P("dp", "seq", "tp"),
            P("tp", None),
            P("tp"),
            P("tp", "dp"),
            P("dp", "seq", "tp"),
        ),
        out_specs=(
            P("dp", "seq", "tp"),
            P("dp", "seq", "tp"),
            P("dp", "seq", "tp"),
            P("tp", None),
            P("tp"),
            P(("seq", "dp"), "tp"),
        ),
        check_vma=False,
    )
```

profile of v0, /device:TPU:1, one launch (start us, length us, event | category | flops | bytes accessed | tf_op | source)
XLA Modules:
  0.0 1021.1 jit_solution(6205468329109296625)
XLA Ops:
  22.1 6.7 slice.135
  28.8 12.7 %copy.93 = bf16[1024,16,144]{2,1,0:T(8,128)(2,1)} copy(bf16[1024,16,144]{0,2,1:T(8,128)(2,1)} %slice.135) | data formatting | bytes 9437184
  41.5 5.5 all-gather.6.cloned.1.call-done
  47.1 112.5 %all-gather.4.cloned.1.call-done = bf16[1024,4096]{1,0:T(8,128)(2,1)} async-done(((bf16[1024,2048]{1,0:T(8,128)(2,1)}), bf16[1024,4096]{1,0:T(8,128)(2,1)}) %all-gather.4.cloned.1.call-update) | async-done | bytes 8388624 | tf_op jit(solution)/shard_map/all_gather | solution.py:85
  159.6 7.5 fusion.8
  184.4 6.8 slice.120
  191.2 12.5 %copy.92 = bf16[1024,16,144]{2,1,0:T(8,128)(2,1)} copy(bf16[1024,16,144]{0,2,1:T(8,128)(2,1)} %slice.120) | data formatting | bytes 9437184
  215.5 5.8 copy.75
  221.2 5.8 copy.76
  227.0 5.7 copy.77
  232.7 5.7 copy.78
  257.2 35.9 %concatenate.45 = bf16[16,144,1024]{1,0,2:T(8,128)(2,1)} concatenate(bf16[16,16,1024]{1,0,2:T(8,128)(2,1)} %copy.74, bf16[16,16,1024]{1,0,2:T(8,128)(2,1)} %copy.75, bf16[16,16,1024]{1,0,2:T(8,128)(2,1)} %copy.76, bf16[16,16,1024]{1,0,2:T(8,128)(2,1)} %copy.77, bf16[16,16,1024]{1,0,2:T(8,128)(2,1)} %copy.78, bf16[16,16,1024]{1,0,2:T(8,128)(2,1)} %copy.79, ...), dimensions={1} | concatenate | bytes 9437184 | tf_op jit(solution)/shard_map/concatenate | solution.py:48
  293.1 11.3 %convolution_bitcast_fusion.1 = f32[16,16,1024]{1,0,2:T(8,128)} fusion(bf16[16,144,1024]{1,0,2:T(8,128)(2,1)} %concatenate.45, bf16[1024,16,144]{2,1,0:T(8,128)(2,1)} %copy.93), kind=kOutput, calls=%fused_computation.2 | convolution fusion | flops 75497472 | bytes 10485760 | tf_op jit(solution)/shard_map/cab,ibc->iac/dot_general | solution.py:94
  304.4 5.1 copy.85
  311.4 5.7 copy.62
  317.1 5.7 copy.63
  322.8 5.8 copy.64
  328.6 5.7 copy.65
  334.4 5.9 copy.66
  340.3 5.7 copy.67
  355.4 35.9 %concatenate.41 = bf16[16,144,1024]{1,0,2:T(8,128)(2,1)} concatenate(bf16[16,16,1024]{1,0,2:T(8,128)(2,1)} %copy.62, bf16[16,16,1024]{1,0,2:T(8,128)(2,1)} %copy.63, bf16[16,16,1024]{1,0,2:T(8,128)(2,1)} %copy.64, bf16[16,16,1024]{1,0,2:T(8,128)(2,1)} %copy.65, bf16[16,16,1024]{1,0,2:T(8,128)(2,1)} %copy.66, bf16[16,16,1024]{1,0,2:T(8,128)(2,1)} %copy.67, ...), dimensions={1} | concatenate | bytes 9437184 | tf_op jit(solution)/shard_map/concatenate | solution.py:48
  391.4 9.9 fusion.29
  401.2 11.3 %convolution_bitcast_fusion.2 = f32[16,16,1024]{1,0,2:T(8,128)} fusion(bf16[16,144,1024]{1,0,2:T(8,128)(2,1)} %concatenate.41, bf16[1024,16,144]{2,1,0:T(8,128)(2,1)} %copy.92), kind=kOutput, calls=%fused_computation.3 | convolution fusion | flops 75497472 | bytes 10485760 | tf_op jit(solution)/shard_map/cab,ibc->iac/dot_general | solution.py:73
  417.6 15.0 %copy.87 = f32[1024,16,144]{0,2,1:T(8,128)} copy(f32[1024,16,144]{2,1,0:T(8,128)} %fusion.29) | data formatting | bytes 18874368 | tf_op jit(solution)/shard_map/iac,ibc->cab/dot_general | solution.py:104
  432.6 9.3 concatenate.47
  441.9 10.3 %reshape.126 = f32[1024,16,145]{0,2,1:T(8,128)} reshape(f32[1024,2320]{0,1:T(8,128)} %concatenate.47) | data formatting | bytes 19005440 | tf_op jit(solution)/shard_map/reshape | solution.py:55
  452.2 5.5 slice_reduce_fusion
  466.4 8.1 convolution_bitcast_fusion
  474.5 17.5 %copy.90 = f32[4096,1024]{1,0:T(8,128)} copy(f32[4096,1024]{0,1:T(8,128)} %convolution_bitcast_fusion) | data formatting | bytes 33554432
  492.0 125.5 %psum.15 = f32[1024]{0:T(1024)S(1)} all-reduce(f32[1024]{0:T(1024)S(1)} %get-tuple-element.24), channel_id=1, replica_groups=mesh['seq'=32,'tp'=4,'dp'=2] {'seq','dp'}, use_global_device_ids=true, to_apply=%region_3.0 | all-reduce | flops 1024 | bytes 8192 | tf_op jit(solution)/shard_map/psum | solution.py:108
  618.0 24.0 %all-reduce.3.cloned.1.call-done = f32[1024,128]{0,1:T(8,128)} async-done(((f32[1024,128]{0,1:T(8,128)}), f32[1024,128]{0,1:T(8,128)}) %all-reduce.3.cloned.1.call-update) | async-done | bytes 524304 | tf_op jit(solution)/shard_map/psum | solution.py:108
  644.1 367.9 %reduce-scatter.4.cloned.1.call-done = f32[64,1024]{1,0:T(8,128)} async-done(((f32[4096,1024]{1,0:T(8,128)}), f32[64,1024]{1,0:T(8,128)}) %reduce-scatter.4.cloned.1.call-update) | async-done | bytes 262160
  (61 shorter events, 92.6 us)
Async XLA Ops:
  7.2 39.9 %all-gather.6.cloned.1.call-start = ((), (), s32[]{:S(2)}) async-start(), calls=%async_computation.3 | async-start | bytes 2621440 | tf_op jit(solution)/shard_map/all_gather | solution.py:81
  7.9 151.7 %all-gather.4.cloned.1.call-start = ((), (), s32[]{:S(2)}) async-start(), calls=%async_computation.1 | async-start | bytes 12582912 | tf_op jit(solution)/shard_map/all_gather | solution.py:85
  8.6 633.4 %all-reduce.3.cloned.1.call-start = ((), (), s32[]{:S(2)}) async-start(), calls=%async_computation.2 | async-start | bytes 1048576 | tf_op jit(solution)/shard_map/psum | solution.py:108
  28.8 130.8 %copy-start = (bf16[1,256,1024]{2,1,0:T(8,128)(2,1)S(1)}, bf16[1,256,1024]{2,1,0:T(8,128)(2,1)}, u32[]{:S(2)}) copy-start(bf16[1,256,1024]{2,1,0:T(8,128)(2,1)} %param.9) | copy-start | bytes 1572868
  28.8 130.8 %copy-start.1 = (bf16[1,256,1024]{2,1,0:T(8,128)(2,1)S(1)}, bf16[1,256,1024]{2,1,0:T(8,128)(2,1)}, u32[]{:S(2)}) copy-start(bf16[1,256,1024]{2,1,0:T(8,128)(2,1)} %param.8) | copy-start | bytes 1572868
  28.8 130.8 %copy-start.3 = (bf16[1,256,1024]{2,1,0:T(8,128)(2,1)S(1)}, bf16[1,256,1024]{2,1,0:T(8,128)(2,1)}, u32[]{:S(2)}) copy-start(bf16[1,256,1024]{2,1,0:T(8,128)(2,1)} %param.7) | copy-start | bytes 1572868
  167.8 44.8 %collective-permute-start.1 = (bf16[127,1024]{1,0:T(8,128)(2,1)}, bf16[127,1024]{1,0:T(8,128)(2,1)}, u32[]{:S(2)}, u32[]{:S(2)}) collective-permute-start(bf16[127,1024]{1,0:T(8,128)(2,1)} %slice.121), channel_id=1, source_target_pairs={{8,0},{16,8},{24,16},{32,24},{40,32},{48,40},{56,48},{64,56},{72,6... | collective-permute-start | bytes 780296 | tf_op jit(solution)/shard_map/ppermute | solution.py:14
  209.3 100.2 %collective-permute-start = (bf16[127,1024]{1,0:T(8,128)(2,1)}, bf16[127,1024]{1,0:T(8,128)(2,1)S(1)}, u32[]{:S(2)}, u32[]{:S(2)}) collective-permute-start(bf16[127,1024]{1,0:T(8,128)(2,1)} %slice.106), channel_id=1, source_target_pairs={{0,8},{8,16},{16,24},{24,32},{32,40},{40,48},{48,56},{56,64},{64,7... | collective-permute-start | bytes 780296 | tf_op jit(solution)/shard_map/ppermute | solution.py:14
  452.2 10.6 %copy-start.4 = (f32[1024]{0:T(1024)S(1)}, f32[1024]{0:T(1024)}, u32[]{:S(2)}) copy-start(f32[1024]{0:T(1024)} %param.11) | copy-start | bytes 12292
  462.5 549.5 %reduce-scatter.4.cloned.1.call-start = ((), (), s32[]{:S(2)}) async-start(), calls=%async_computation.4 | async-start | bytes 17039360
  462.8 3.5 copy-start.2
Sparse Core Ops, SparseCore 0:
  9.8 37.1 all-gather.5
  48.8 110.6 all-gather.3
  462.6 179.3 all-reduce.2
  644.4 367.5 reduce-scatter.3
where the time goes:
time: 1030 us; the launch traced here: 1020 us
  waiting for transfers between devices  511 us (50%)
  local copies, waits for them, and re-layouts  298 us (29%)
  blocking collectives  125 us (12%)
  matrix products  48 us (5%)
  other arithmetic  17.2 us (2%)
  between operations  14.4 us (1%)
    unnamed x5, waiting for transfers between devices  369 us
    psum x1, blocking collectives, per_device(): lax.psum((lag_sums(blocks, tap_count), skip_term), ('seq', 'dp'))  125 us
    all_gather x1, waiting for transfers between devices, per_device(): lax.all_gather(out_weight, 'dp', axis=1, tiled=True)  113 us
    reshape x17, local copies, waits for them, and re-layouts, windows(): extended[lower:lower + length]  90.5 us
    concatenate x2, local copies, waits for them, and re-layouts, windows(): return jnp.concatenate(pieces, axis=1)  71.9 us
    unnamed x16, local copies, waits for them, and re-layouts  45.8 us
    psum x1, waiting for transfers between devices, per_device(): lax.psum((lag_sums(blocks, tap_count), skip_term), ('seq', 'dp'))  24 us
  transfers between devices with their start and end apart: 6, of which 4 were waited for; matrix products, arithmetic and copies ran while one was open for 20% of the time, Pallas kernels for 0%

commit v1 on v0

v1 whole, which is shorter than its diff:
```python
import itertools
import math

import jax
import jax.numpy as jnp
import ml_dtypes
import numpy as np
from jax import lax
from jax.experimental import pallas as pl
from jax.experimental.pallas import tpu as pltpu
from jax.sharding import PartitionSpec as P

ROWS = 256
TAPS = 128
SIZE = ROWS + TAPS
HALF = SIZE // 2
CHANNELS = 1024
TILE = 256
COPIES = 200
BF16 = jnp.bfloat16
F32 = jnp.float32


def split_table(table):
    high = table.astype(ml_dtypes.bfloat16)
    low = (table - high.astype(np.float64)).astype(ml_dtypes.bfloat16)
    return np.stack([high, low])


def spectrum_tables():
    odd = 2 * np.arange(HALF) + 1

    def angles(positions):
        return np.pi * ((odd[:, None] * positions[None, :]) % (2 * SIZE)) / SIZE

    ahead = angles(np.arange(SIZE))
    forward = np.concatenate([np.cos(ahead), -np.sin(ahead)], axis=0)
    places = np.concatenate(
        [np.arange(TAPS, SIZE), np.arange(ROWS), np.arange(-TAPS, 0)]
    )
    behind = angles(places).T
    inverse = (2.0 / SIZE) * np.concatenate([np.cos(behind), -np.sin(behind)], axis=1)
    return split_table(forward), split_table(inverse)


def matmul(left, right):
    return jnp.dot(left, right, preferred_element_type=F32)


def matmul_nt(left, right):
    return lax.dot_general(
        left, right, (((1,), (1,)), ((), ())), preferred_element_type=F32
    )


def y_near(y):
    return (1 - y[0], y[1])


def y_far(y):
    return (1 - y[0], 1 - y[1])


def z_up(z):
    return z + 1 - 2 * lax.rem(z, 2)


def z_down(z):
    return lax.rem(z + 2 * lax.rem(z, 2) + 7, 8)


def z_three(z):
    return lax.rem(z + 11 - 6 * lax.rem(z, 2), 8)


def z_back_three(z):
    return lax.rem(z + 5 + 6 * lax.rem(z, 2), 8)


PLANS = (
    (("y", y_near), ("y", y_far), ("z", z_up), ("z", z_down), ("z", z_three)),
    (("y", y_far), ("y", y_near), ("z", z_down), ("z", z_up), ("z", z_back_three)),
    (("z", z_up), ("z", z_down), ("y", y_near), ("y", y_far), ("z", z_three)),
    (("z", z_down), ("z", z_up), ("y", y_far), ("y", y_near), ("z", z_back_three)),
)


def kept(rest, place):
    if not rest:
        return [place]
    return kept(rest[1:], place) + kept(rest[1:], rest[0](place))


def remaining(plan, step, axis):
    return [move for name, move in plan[step + 1 :] if name == axis]


def slots(plan, step, y, z):
    y_rest, z_rest = remaining(plan, step, "y"), remaining(plan, step, "z")
    y_list = [None] if len(y_rest) == 2 else kept(y_rest, y)
    z_list = [None] if len(z_rest) == 3 else kept(z_rest, z)
    return [(one, other) for one in y_list for other in z_list]


def slot_view(ref, quarter, slot):
    y, z = slot
    if y is None:
        return ref.at[quarter, :, z]
    if z is None:
        return ref.at[quarter, y[0], :, y[1]]
    return ref.at[quarter, y[0], z, y[1]]


def landing_shapes():
    shapes = []
    for plan in PLANS:
        for step in range(5):
            y_rest, z_rest = remaining(plan, step, "y"), remaining(plan, step, "z")
            if len(y_rest) == 2:
                shape = (2 ** len(z_rest), 2, 2, 64, TILE)
            elif len(z_rest) == 3:
                shape = (2 ** len(y_rest), 8, 64, TILE)
            else:
                shape = (2 ** (len(y_rest) + len(z_rest)), 64, TILE)
            shapes.append(shape)
    return shapes


def kernel(
    query, key, value, taps, skip, weight, cot, ahead, behind,
    out_query, out_key, out_value, out_filter, out_weight,
    full_cot, full_weight, turned, turned_away, gated, mixed, mixed_halo, signal, signal_halo,
    tap_spec, mixed_spec, state, grad_gated, partial, lag_sum, lag_out,
    near_land, lag_mid, far_land, send_sem, recv_sem, local_sem, *landing,
):
    seq, tp, dp = lax.axis_index("seq"), lax.axis_index("tp"), lax.axis_index("dp")
    core = lax.rem(seq, 2)
    z = lax.rem(lax.div(seq, 2), 8)
    y = (lax.div(seq, 16), dp)
    scale = 1.0 / math.sqrt(2 * 32 * ROWS)

    def place(y, z, core):
        return ((y[0] * 8 + z) * 2 + core, tp, y[1])

    right, left, across = lax.rem(tp + 1, 4), lax.rem(tp + 3, 4), lax.rem(tp + 2, 4)
    to_right, to_left = (seq, right, dp), (seq, left, dp)
    to_next, to_prior = (lax.rem(seq + 1, 32), tp, dp), (lax.rem(seq + 31, 32), tp, dp)
    to_core = place(y, z, 1 - core)
    member = (y[1] * 2 + y[0]) * 2 + core

    def to_member(index):
        high = lax.div(index, 4)
        return place((lax.rem(lax.div(index, 2), 2), high), z, lax.rem(index, 2))

    members = [lax.rem(member + i, 8) for i in range(8)]
    heights = [lax.rem(z + i, 8) for i in range(8)]

    barrier = pltpu.get_barrier_semaphore()
    greeted = [to_right, to_left, to_next, to_prior]
    greeted += [to_member(members[i]) for i in range(1, 8)]
    greeted += [place(y, heights[i], core) for i in range(1, 8)]
    for target in greeted:
        pl.semaphore_signal(
            barrier, inc=1, device_id=target, device_id_type=pl.DeviceIdType.MESH
        )
    pl.semaphore_wait(barrier, len(greeted))

    numbers = itertools.count()
    started = []

    def send(source, target_ref, target):
        number = next(numbers)
        copy = pltpu.make_async_remote_copy(
            src_ref=source,
            dst_ref=target_ref,
            send_sem=send_sem.at[number],
            recv_sem=recv_sem.at[number],
            device_id=target,
            device_id_type=pl.DeviceIdType.MESH,
        )
        copy.start()
        started.append(copy)
        return copy

    top, bottom = pl.ds(0, 128), pl.ds(128, 128)

    def pass_cot(owner, part, target):
        spot = full_cot.at[owner, part]
        return send(spot, spot, target)

    right_top = send(cot.at[top], full_cot.at[tp, top], to_right)
    left_bottom = send(cot.at[bottom], full_cot.at[tp, bottom], to_left)
    right_bottom = send(cot.at[bottom], full_cot.at[tp, bottom], to_right)
    left_top = send(cot.at[top], full_cot.at[tp, top], to_left)

    pieces = [(i, r) for r in range(2) for i in range(2)]
    given_row = ((1 - y[0]) * 2 + core) * 256
    taken_row = (y[0] * 2 + core) * 256
    near_row = ((1 - y[0]) * 2 + core) * 256

    def weight_spot(owner, row, piece):
        i, r = piece
        return full_weight.at[owner * 2 + i, pl.ds(pl.multiple_of(row + r * 128, 128), 128)]

    imports = []
    for i, r in pieces:
        source = weight.at[
            pl.ds(pl.multiple_of(given_row + r * 128, 128), 128), pl.ds(i * 1024, 1024)
        ]
        imports.append(send(source, weight_spot(dp, given_row, (i, r)), place(y_far(y), z, core)))

    own = [
        pltpu.make_async_copy(
            weight.at[:, pl.ds(i * 1024, 1024)], full_weight.at[dp * 2 + i], local_sem.at[i]
        )
        for i in range(2)
    ]
    for copy in own:
        copy.start()

    mixed[...] = (key[...].astype(F32) * value[...].astype(F32)).astype(BF16)
    mixed_sent = send(mixed.at[bottom], mixed_halo, to_next)
    full_cot[tp] = cot[...]

    def turn(owner):
        for i in range(4):
            mine = pl.ds(pl.multiple_of((i * 2 + core) * 128, 128), 128)
            other = pl.ds(pl.multiple_of((i * 2 + 1 - core) * 128, 128), 128)
            turned[owner * 4 + i, :, pl.ds(0, ROWS)] = full_cot[owner, :, mine].T
            turned_away[owner * 4 + i] = full_cot[owner, :, other].T
        group = pl.ds(owner * 4, 4)
        return send(turned_away.at[group], turned.at[group, :, pl.ds(ROWS, ROWS)], to_core)

    turns = [turn(tp)]

    def columns(tile):
        return pl.ds(pl.multiple_of(tile * TILE, TILE), TILE)

    def spectrum(part, block):
        return matmul(ahead[0, :, part], block) + matmul(ahead[1, :, part], block)

    def restore(places, real, imag):
        spec = jnp.concatenate([real, imag], axis=0)
        high = spec.astype(BF16)
        low = (spec - high.astype(F32)).astype(BF16)
        table = behind[0, places]
        return matmul(table, high) + matmul(behind[1, places], high) + matmul(table, low)

    @pl.loop(0, CHANNELS // TILE)
    def _(tile):
        cols = columns(tile)
        block = taps[cols]
        spec = matmul_nt(ahead[0, :, pl.ds(0, TAPS)], block)
        spec = spec + matmul_nt(ahead[1, :, pl.ds(0, TAPS)], block)
        tap_spec[pl.ds(0, HALF), cols] = spec[:HALF] + skip[:, cols]
        tap_spec[pl.ds(HALF, HALF), cols] = spec[HALF:]
        mixed_spec[:, cols] = spectrum(pl.ds(TAPS, ROWS), mixed[:, cols])

    right_top.wait_recv()
    forward_right = pass_cot(left, top, to_right)
    left_bottom.wait_recv()
    forward_left = pass_cot(right, bottom, to_left)

    to_near = place(y_near(y), z, core)
    near_copies, core_copies = [], []

    def share_import(number):
        imports[number].wait_recv()
        spot = weight_spot(1 - dp, taken_row, pieces[number])
        near_copies.append(send(spot, spot, to_near))
        core_copies.append(send(spot, spot, to_core))

    mixed_sent.wait_recv()

    @pl.loop(0, CHANNELS // TILE)
    def _(tile):
        cols = columns(tile)
        halo = jnp.where(seq > 0, mixed_halo[:, cols], jnp.zeros((TAPS, TILE), BF16))
        spec = mixed_spec[:, cols] + spectrum(pl.ds(0, TAPS), halo)
        real, imag = spec[:HALF], spec[HALF:]
        tap_real, tap_imag = tap_spec[pl.ds(0, HALF), cols], tap_spec[pl.ds(HALF, HALF), cols]
        value_now = restore(
            pl.ds(0, ROWS),
            real * tap_real - imag * tap_imag,
            real * tap_imag + imag * tap_real,
        )
        state[:, cols] = value_now
        gated[pl.ds(0, ROWS), cols] = (query[:, cols].astype(F32) * value_now).astype(BF16)

    gated_sent = send(gated.at[pl.ds(0, ROWS)], gated.at[pl.ds(ROWS, ROWS)], to_core)
    share_import(0)
    right_bottom.wait_recv()
    turns.append(turn(left))
    share_import(1)
    left_top.wait_recv()
    turns.append(turn(right))
    share_import(2)
    forward_right.wait_recv()
    forward_left.wait_recv()
    turns.append(turn(across))
    share_import(3)

    for copy in turns:
        copy.wait_recv()
    gated_sent.wait_recv()

    def exchange(quarter, step):
        axis, move = PLANS[quarter][step]
        there_y = move(y) if axis == "y" else y
        there_z = move(z) if axis == "z" else z
        landed = landing[quarter * 5 + step]
        return [
            send(slot_view(partial, quarter, slot), landed.at[i], place(there_y, there_z, core))
            for i, slot in enumerate(slots(PLANS[quarter], step, there_y, there_z))
        ]

    rounds = []
    for quarter in range(4):

        @pl.loop(0, 4)
        def _(part):
            rows = turned[pl.ds(part * 4, 4)].reshape(512, 2 * ROWS)
            block = matmul(rows, gated[:, pl.ds(quarter * TILE, TILE)]).astype(BF16)
            partial[
                quarter, lax.div(part, 2), pl.ds(lax.rem(part, 2) * 4, 4)
            ] = block.reshape(4, 2, 64, TILE)

        rounds.append(exchange(quarter, 0))

    def pass_near(number):
        near_copies[number].wait_recv()
        spot = weight_spot(1 - dp, near_row, pieces[number])
        core_copies.append(send(spot, spot, to_core))

    for number in range(4):
        pass_near(number)
    for copy in own:
        copy.wait()
    for copy in core_copies:
        copy.wait_recv()

    @pl.loop(0, CHANNELS // TILE)
    def _(tile):
        cols = columns(tile)
        total = matmul_nt(full_cot[0], full_weight[0, cols])
        for owner in range(1, 4):
            total = total + matmul_nt(full_cot[owner], full_weight[owner, cols])
        out_query[:, cols] = (total * state[:, cols]).astype(BF16)
        signal[:, cols] = (total * query[:, cols].astype(F32)).astype(BF16)

    signal_sent = send(signal.at[top], signal_halo, to_prior)

    def combine(quarter, step):
        for copy in rounds[quarter]:
            copy.wait_recv()
        landed = landing[quarter * 5 + step]
        for i, slot in enumerate(slots(PLANS[quarter], step, y, z)):
            view = slot_view(partial, quarter, slot)
            total = view[...].astype(F32) + landed[i].astype(F32)
            if step < 4:
                view[...] = total.astype(BF16)
            else:
                out_weight[:, pl.ds(quarter * TILE, TILE)] = total * scale
        if step < 4:
            rounds[quarter] = exchange(quarter, step + 1)

    for quarter in range(4):
        combine(quarter, 0)

    signal_sent.wait_recv()

    @pl.loop(0, CHANNELS // TILE)
    def _(tile):
        cols = columns(tile)
        halo = jnp.where(seq < 31, signal_halo[:, cols], jnp.zeros((TAPS, TILE), BF16))
        spec = spectrum(pl.ds(0, ROWS), signal[:, cols]) + spectrum(pl.ds(ROWS, TAPS), halo)
        real, imag = spec[:HALF], spec[HALF:]
        part_real, part_imag = mixed_spec[pl.ds(0, HALF), cols], mixed_spec[pl.ds(HALF, HALF), cols]
        lags = restore(
            pl.ds(2 * ROWS, TAPS),
            real * part_real + imag * part_imag,
            imag * part_real - real * part_imag,
        )
        for i in range(TILE // 128):
            block = lags[:, i * 128 : (i + 1) * 128].T
            lag_sum[tile * (TILE // 128) + i] = block.astype(BF16)
        tap_real, tap_imag = tap_spec[pl.ds(0, HALF), cols], tap_spec[pl.ds(HALF, HALF), cols]
        back = restore(
            pl.ds(ROWS, ROWS),
            real * tap_real + imag * tap_imag,
            imag * tap_real - real * tap_imag,
        )
        out_key[:, cols] = (back * value[:, cols].astype(F32)).astype(BF16)
        out_value[:, cols] = (back * key[:, cols].astype(F32)).astype(BF16)

    copies = [
        send(lag_sum.at[members[i]], near_land.at[i - 1], to_member(members[i])) for i in range(1, 8)
    ]
    for quarter in range(4):
        combine(quarter, 1)
    for copy in copies:
        copy.wait_recv()
    total = lag_sum[member].astype(F32)
    for i in range(7):
        total = total + near_land[i].astype(F32)
    lag_mid[...] = total.reshape(8, 16, TAPS)
    copies = [
        send(lag_mid.at[heights[i]], far_land.at[i - 1], place(y, heights[i], core))
        for i in range(1, 8)
    ]
    for quarter in range(4):
        combine(quarter, 2)
    for copy in copies:
        copy.wait_recv()
    total = lag_mid[z]
    for i in range(7):
        total = total + far_land[i]
    lag_out[member, z] = total * scale
    mine = lag_out.at[member, z]
    copies = [send(mine, mine, place(y, heights[i], core)) for i in range(1, 8)]
    for quarter in range(4):
        combine(quarter, 3)
    for copy in copies:
        copy.wait_recv()
    mine = lag_out.at[member]
    copies = [send(mine, mine, to_member(members[i])) for i in range(1, 8)]
    for quarter in range(4):
        combine(quarter, 4)
    for copy in copies:
        copy.wait_recv()
    out_filter[...] = lag_out[...]
    for copy in started:
        copy.wait_send()


def per_device(query_gate, key_gate, value_input, filter_taps, skip_gain, out_weight, cotangent):
    ahead, behind = spectrum_tables()
    vmem = pl.BlockSpec(memory_space=pltpu.VMEM)
    scratch = [
        ((4, ROWS, 1024), BF16),
        ((4, CHANNELS, 1024), BF16),
        ((16, 128, 2 * ROWS), BF16),
        ((16, 128, ROWS), BF16),
        ((2 * ROWS, CHANNELS), BF16),
        ((ROWS, CHANNELS), BF16),
        ((TAPS, CHANNELS), BF16),
        ((ROWS, CHANNELS), BF16),
        ((TAPS, CHANNELS), BF16),
        ((SIZE, CHANNELS), F32),
        ((SIZE, CHANNELS), F32),
        ((ROWS, CHANNELS), F32),
        ((8, 128), F32),
        ((4, 2, 8, 2, 64, TILE), BF16),
        ((8, 128, TAPS), BF16),
        ((8, 8, 16, TAPS), F32),
        ((7, 128, TAPS), BF16),
        ((8, 16, TAPS), F32),
        ((7, 16, TAPS), F32),
    ]
    grad_query, grad_key, grad_value, grad_filter, grad_weight = pl.pallas_call(
        kernel,
        out_shape=(
            jax.ShapeDtypeStruct((ROWS, CHANNELS), BF16),
            jax.ShapeDtypeStruct((ROWS, CHANNELS), BF16),
            jax.ShapeDtypeStruct((ROWS, CHANNELS), BF16),
            jax.ShapeDtypeStruct((8, 8, 16, TAPS), F32),
            jax.ShapeDtypeStruct((64, CHANNELS), F32),
        ),
        in_specs=[vmem] * 5 + [pl.BlockSpec(memory_space=pl.ANY)] + [vmem] * 3,
        out_specs=[vmem] * 5,
        scratch_shapes=[pltpu.VMEM(shape, dtype) for shape, dtype in scratch]
        + [
            pltpu.SemaphoreType.DMA((COPIES,)),
            pltpu.SemaphoreType.DMA((COPIES,)),
            pltpu.SemaphoreType.DMA((2,)),
        ]
        + [pltpu.VMEM(shape, BF16) for shape in landing_shapes()],
        compiler_params=pltpu.CompilerParams(
            collective_id=0, has_side_effects=True, vmem_limit_bytes=56 * 1024 * 1024
        ),
    )(
        query_gate[0], key_gate[0], value_input[0], filter_taps, skip_gain[None, :],
        out_weight, cotangent[0], jnp.asarray(ahead), jnp.asarray(behind),
    )
    grad_filter = grad_filter.reshape(CHANNELS, TAPS)
    return (
        grad_query[None],
        grad_key[None],
        grad_value[None],
        grad_filter,
        grad_filter[:, 0],
        grad_weight,
    )


def solution(mesh):
    return jax.shard_map(
        per_device,
        mesh=mesh,
        in_specs=(
            P("dp", "seq", "tp"),
            P("dp", "seq", "tp"),
            P("dp", "seq", "tp"),
            P("tp", None),
            P("tp"),
            P("tp", "dp"),
            P("dp", "seq", "tp"),
        ),
        out_specs=(
            P("dp", "seq", "tp"),
            P("dp", "seq", "tp"),
            P("dp", "seq", "tp"),
            P("tp", None),
            P("tp"),
            P(("seq", "dp"), "tp"),
        ),
        check_vma=False,
    )
```

time: 1030 us -> 104 us (0.10)
  waiting for transfers between devices: 511 us -> 0 us
  local copies, waits for them, and re-layouts: 298 us -> 10.1 us
  blocking collectives: 125 us -> 0 us
  Pallas kernels: 0 us -> 93.4 us
  matrix products: 48 us -> 0 us
  other arithmetic: 17.2 us -> 0 us
  between operations: 14.4 us -> 0.65 us
    unnamed x5 -> x0, waiting for transfers between devices: 369 us -> none
    psum x1 -> x0, blocking collectives: 125 us -> none  [per_device(): lax.psum((lag_sums(blocks, tap_count), skip_term), ('seq', 'dp'))]
    all_gather x2 -> x0, waiting for transfers between devices: 118 us -> none  [the longest x1 113 us: per_device(): lax.all_gather(out_weight, 'dp', axis=1, tiled=True)]
    reshape x20 -> x0, local copies, waits for them, and re-layouts: 111 us -> none  [the longest x17 90.5 us: windows(): extended[lower:lower + length]]
    pallas_call x0 -> x1, Pallas kernels: none -> 93.4 us  [per_device(): pl.pallas_call(kernel, out_shape=(jax.ShapeDtypeStruct((ROWS, CHANNELS),...]
    concatenate x7 -> x0, local copies, waits for them, and re-layouts: 81.6 us -> none  [the longest x2 71.9 us: windows(): return jnp.concatenate(pieces, axis=1)]
    dot_general x5 -> x0, matrix products: 48 us -> none  [the longest x1 11.3 us: per_device(): jnp.einsum('cab,ibc->iac', backward_table(filter_taps), windows(signal_ex...]
    unnamed x16 -> x7, local copies, waits for them, and re-layouts: 45.8 us -> 8.18 us
  transfers between devices with their start and end apart: 6 -> 0, of which waited for: 4 -> 0; matrix products, arithmetic and copies ran while one was open for 20% -> 0% of each run, Pallas kernels for 0% -> 0%
where the time goes in v1:
time: 104 us
  Pallas kernels  93.4 us (90%)
  local copies, waits for them, and re-layouts  10.1 us (10%)
    pallas_call x1, Pallas kernels, per_device(): pl.pallas_call(kernel, out_shape=(jax.ShapeDtypeStruct((ROWS, CHANNELS),...  93.4 us
    unnamed x7, local copies, waits for them, and re-layouts  8.18 us

profile of v1, /device:TPU:1, one launch (start us, length us, event | category | flops | bytes accessed | tf_op | source)
XLA Modules:
  0.0 104.1 jit_solution(8749063153170321831)
XLA Ops:
  0.6 93.4 %shard_map.136 = (bf16[256,1024]{1,0:T(8,128)(2,1)}, bf16[256,1024]{1,0:T(8,128)(2,1)}, bf16[256,1024]{1,0:T(8,128)(2,1)}, f32[8,8,16,128]{3,2,1,0:T(8,128)}, f32[64,1024]{1,0:T(8,128)}) custom-call(bf16[256,1024]{1,0:T(8,128)(2,1)} %bitcast.11, bf16[256,1024]{1,0:T(8,128)(2,1)} %bitcast.12, bf16[256,1024]{1,0:T(8,128)(2,1)} %bitcast.13, ...), custom_call_target="tpu_custom_call" | custom-call | tf_op jit(solution)/shard_map/pallas_call | solution.py:460
  94.0 0.0 copy-start
  94.0 1.9 %slice_reduce_fusion = f32[1024]{0:T(1024)} fusion(f32[1024,128]{1,0:T(8,128)} %bitcast.9), kind=kLoop, calls=%fused_computation | loop fusion | bytes 8192 | tf_op jit(solution)/shard_map/slice | solution.py:491
  95.9 1.9 %copy.20 = bf16[1,256,1024]{2,1,0:T(8,128)(2,1)} copy(bf16[1,256,1024]{2,1,0:T(8,128)(2,1)} %bitcast.17) | data formatting | bytes 1048576
  97.8 1.9 %copy.21 = bf16[1,256,1024]{2,1,0:T(8,128)(2,1)} copy(bf16[1,256,1024]{2,1,0:T(8,128)(2,1)} %bitcast.16) | data formatting | bytes 1048576
  99.6 1.9 %copy.22 = bf16[1,256,1024]{2,1,0:T(8,128)(2,1)} copy(bf16[1,256,1024]{2,1,0:T(8,128)(2,1)} %bitcast.15) | data formatting | bytes 1048576
  101.5 1.9 %copy.23 = f32[1024,128]{1,0:T(8,128)} copy(f32[1024,128]{1,0:T(8,128)} %bitcast.10) | data formatting | bytes 1048576
  103.4 0.0 copy-done
  103.4 0.7 copy.24
Async XLA Ops:
  94.0 9.4 %copy-start = (f32[64,1024]{1,0:T(8,128)S(1)}, f32[64,1024]{1,0:T(8,128)}, u32[]{:S(2)}) copy-start(f32[64,1024]{1,0:T(8,128)} %get-tuple-element.27) | copy-start | bytes 786436

commit v2 on v1

v2 whole, which is shorter than its diff:
```python
import itertools
import math

import jax
import jax.numpy as jnp
import ml_dtypes
import numpy as np
from jax import lax
from jax.experimental import pallas as pl
from jax.experimental.pallas import tpu as pltpu
from jax.sharding import PartitionSpec as P

ROWS = 256
TAPS = 128
SIZE = ROWS + TAPS
HALF = SIZE // 2
CHANNELS = 1024
TILE = 256
COPIES = 131
BF16 = jnp.bfloat16
F32 = jnp.float32


def split_table(table):
    high = table.astype(ml_dtypes.bfloat16)
    low = (table - high.astype(np.float64)).astype(ml_dtypes.bfloat16)
    return np.stack([high, low])


def spectrum_tables():
    odd = 2 * np.arange(HALF) + 1

    def angles(positions):
        return np.pi * ((odd[:, None] * positions[None, :]) % (2 * SIZE)) / SIZE

    ahead = angles(np.arange(SIZE))
    forward = np.concatenate([np.cos(ahead), -np.sin(ahead)], axis=0)
    places = np.concatenate(
        [np.arange(TAPS, SIZE), np.arange(ROWS), np.arange(-TAPS, 0)]
    )
    behind = angles(places).T
    inverse = (2.0 / SIZE) * np.concatenate([np.cos(behind), -np.sin(behind)], axis=1)
    return split_table(forward), split_table(inverse)


def matmul(left, right):
    return jnp.dot(left, right, preferred_element_type=F32)


def matmul_nt(left, right):
    return lax.dot_general(
        left, right, (((1,), (1,)), ((), ())), preferred_element_type=F32
    )


def y_near(y):
    return (1 - y[0], y[1])


def y_far(y):
    return (1 - y[0], 1 - y[1])


def z_up(z):
    return z + 1 - 2 * lax.rem(z, 2)


def z_down(z):
    return lax.rem(z + 2 * lax.rem(z, 2) + 7, 8)


def z_three(z):
    return lax.rem(z + 11 - 6 * lax.rem(z, 2), 8)


def z_back_three(z):
    return lax.rem(z + 5 + 6 * lax.rem(z, 2), 8)


PLANS = (
    (("y", y_near), ("y", y_far), ("z", z_up), ("z", z_down), ("z", z_three)),
    (("y", y_far), ("y", y_near), ("z", z_down), ("z", z_up), ("z", z_back_three)),
    (("z", z_up), ("z", z_down), ("y", y_near), ("y", y_far), ("z", z_three)),
    (("z", z_down), ("z", z_up), ("y", y_far), ("y", y_near), ("z", z_back_three)),
)


def kept(rest, place):
    if not rest:
        return [place]
    return kept(rest[1:], place) + kept(rest[1:], rest[0](place))


def remaining(plan, step, axis):
    return [move for name, move in plan[step + 1 :] if name == axis]


def slots(plan, step, y, z):
    y_rest, z_rest = remaining(plan, step, "y"), remaining(plan, step, "z")
    y_list = [None] if len(y_rest) == 2 else kept(y_rest, y)
    z_list = [None] if len(z_rest) == 3 else kept(z_rest, z)
    return [(one, other) for one in y_list for other in z_list]


def slot_view(ref, quarter, slot):
    y, z = slot
    if y is None:
        return ref.at[quarter, :, z]
    if z is None:
        return ref.at[quarter, y[0], :, y[1]]
    return ref.at[quarter, y[0], z, y[1]]


def landing_shapes():
    shapes = []
    for plan in PLANS:
        for step in range(5):
            y_rest, z_rest = remaining(plan, step, "y"), remaining(plan, step, "z")
            if step == 0:
                shape = (4, 4, 64, TILE) if plan[0][0] == "y" else (4, 2, 2, 64, TILE)
            elif len(y_rest) == 2:
                shape = (2 ** len(z_rest), 2, 2, 64, TILE)
            elif len(z_rest) == 3:
                shape = (2 ** len(y_rest), 8, 64, TILE)
            else:
                shape = (2 ** (len(y_rest) + len(z_rest)), 64, TILE)
            shapes.append(shape)
    return shapes


def first_slots(quarter, owner, y, z, keep):
    low, half = lax.div(owner, 2), lax.rem(owner, 2)
    group = pl.ds(half * 4, 4)
    other = 0 if keep else 1
    if quarter == 0:
        return [(low, group, lax.rem(y[1] + y[0] + low + other, 2))]
    if quarter == 1:
        return [(low, group, lax.rem(y[1] + other, 2))]
    if quarter == 2:
        kind = lax.rem(lax.div(lax.rem(z, 4) + 1, 2) + other, 2)
        return [(low, half * 4 + kind + i * (3 - 2 * kind)) for i in range(2)]
    kind = lax.rem(lax.div(lax.rem(z, 4), 2) + other, 2)
    return [(low, half * 4 + kind * 2 + i) for i in range(2)]


def kernel(
    query_in, key_in, value_in, taps_in, skip_in, weight, cot, ahead_in, behind_in,
    query_out, key_out, value_out, filter_out, skip_out, weight_out,
    query, key, value, taps, skip, ahead, behind,
    full_cot, full_weight, turned, turned_away, gated, mixed, mixed_halo, signal, signal_halo,
    tap_spec, mixed_spec, signal_spec, state, grad_gated, partial, lag_sum, lag_out,
    near_land, lag_mid, far_land, lag_last, made_query, made_key, made_value, made_filter,
    made_skip, made_weight, send_sem, recv_sem, local_sem, *landing,
):
    seq, tp, dp = lax.axis_index("seq"), lax.axis_index("tp"), lax.axis_index("dp")
    core = lax.rem(seq, 2)
    z = lax.rem(lax.div(seq, 2), 8)
    y = (lax.div(seq, 16), dp)
    scale = 1.0 / math.sqrt(2 * 32 * ROWS)

    def place(y, z, core):
        return ((y[0] * 8 + z) * 2 + core, tp, y[1])

    right, left, across = lax.rem(tp + 1, 4), lax.rem(tp + 3, 4), lax.rem(tp + 2, 4)
    to_right, to_left = (seq, right, dp), (seq, left, dp)
    to_next, to_prior = (lax.rem(seq + 1, 32), tp, dp), (lax.rem(seq + 31, 32), tp, dp)
    to_core = place(y, z, 1 - core)
    to_near, to_far = place(y_near(y), z, core), place(y_far(y), z, core)
    to_side = [place(y, z_up(z), core), place(y, z_down(z), core)]
    member = (y[1] * 2 + y[0]) * 2 + core

    def to_member(index):
        high = lax.div(index, 4)
        return place((lax.rem(lax.div(index, 2), 2), high), z, lax.rem(index, 2))

    members = [lax.rem(member + i, 8) for i in range(8)]
    heights = [lax.rem(z + i, 8) for i in range(8)]

    barrier = pltpu.get_barrier_semaphore()
    greeted = [to_right, to_left, to_next, to_prior]
    greeted += [to_member(members[i]) for i in range(1, 8)]
    greeted += [place(y, heights[i], core) for i in range(1, 8)]
    for target in greeted:
        pl.semaphore_signal(
            barrier, inc=1, device_id=target, device_id_type=pl.DeviceIdType.MESH
        )

    local_numbers = itertools.count()

    def fetch(source, target):
        copy = pltpu.make_async_copy(source, target, local_sem.at[next(local_numbers)])
        copy.start()
        return copy

    key_copy, value_copy = fetch(key_in, key), fetch(value_in, value)
    cot_copy = fetch(cot, full_cot.at[tp])
    table_copies = [fetch(ahead_in, ahead), fetch(taps_in, taps), fetch(skip_in, skip)]
    state_copies = [fetch(behind_in, behind), fetch(query_in, query)]
    pl.semaphore_wait(barrier, len(greeted))

    numbers = itertools.count()
    started = []

    def send(source, target_ref, target):
        number = next(numbers)
        copy = pltpu.make_async_remote_copy(
            src_ref=source,
            dst_ref=target_ref,
            send_sem=send_sem.at[number],
            recv_sem=recv_sem.at[number],
            device_id=target,
            device_id_type=pl.DeviceIdType.MESH,
        )
        copy.start()
        started.append(copy)
        return copy

    top, bottom = pl.ds(0, 128), pl.ds(128, 128)

    def pass_cot(owner, part, target):
        spot = full_cot.at[owner, part]
        return send(spot, spot, target)

    right_top = send(cot.at[top], full_cot.at[tp, top], to_right)
    left_bottom = send(cot.at[bottom], full_cot.at[tp, bottom], to_left)

    def weight_rows(low, odd, core):
        return pl.ds(pl.multiple_of(((low * 2 + odd) * 2 + core) * 128, 128), 128)

    odd = lax.rem(z, 2)
    given = weight_rows(1 - y[0], odd, core)
    imports = []
    for i in range(2):
        for r in range(2):
            rows = pl.ds(pl.multiple_of(given.start + r * 64, 64), 64)
            source = weight.at[rows, pl.ds(i * 1024, 1024)]
            imports.append(send(source, full_weight.at[dp * 2 + i, rows], to_far))
    right_bottom = send(cot.at[bottom], full_cot.at[tp, bottom], to_right)
    left_top = send(cot.at[top], full_cot.at[tp, top], to_left)
    own = [fetch(weight.at[:, pl.ds(i * 1024, 1024)], full_weight.at[dp * 2 + i]) for i in range(2)]

    key_copy.wait()
    value_copy.wait()
    mixed[...] = (key[...].astype(F32) * value[...].astype(F32)).astype(BF16)
    mixed_sent = send(mixed.at[bottom], mixed_halo, to_next)

    def turn(owner):
        for i in range(4):
            mine = pl.ds(pl.multiple_of((i * 2 + core) * 128, 128), 128)
            other = pl.ds(pl.multiple_of((i * 2 + 1 - core) * 128, 128), 128)
            turned[owner * 4 + i, :, pl.ds(0, ROWS)] = full_cot[owner, :, mine].T
            turned_away[owner * 4 + i] = full_cot[owner, :, other].T
        group = pl.ds(owner * 4, 4)
        return send(turned_away.at[group], turned.at[group, :, pl.ds(ROWS, ROWS)], to_core)

    cot_copy.wait()
    turned_own = turn(tp)

    def columns(tile):
        return pl.ds(pl.multiple_of(tile * TILE, TILE), TILE)

    def spectrum(part, block):
        return matmul(ahead[0, :, part], block) + matmul(ahead[1, :, part], block)

    def restore(places, real, imag):
        spec = jnp.concatenate([real, imag], axis=0)
        high = spec.astype(BF16)
        low = (spec - high.astype(F32)).astype(BF16)
        table = behind[0, places]
        return matmul(table, high) + matmul(behind[1, places], high) + matmul(table, low)

    for copy in table_copies:
        copy.wait()

    @pl.loop(0, CHANNELS // TILE)
    def _(tile):
        cols = columns(tile)
        block = taps[cols]
        spec = matmul_nt(ahead[0, :, pl.ds(0, TAPS)], block)
        spec = spec + matmul_nt(ahead[1, :, pl.ds(0, TAPS)], block)
        tap_spec[pl.ds(0, HALF), cols] = spec[:HALF] + skip[:, cols]
        tap_spec[pl.ds(HALF, HALF), cols] = spec[HALF:]
        mixed_spec[:, cols] = spectrum(pl.ds(TAPS, ROWS), mixed[:, cols])

    for copy in state_copies:
        copy.wait()
    mixed_sent.wait_recv()

    @pl.loop(0, CHANNELS // TILE)
    def _(tile):
        cols = columns(tile)
        halo = jnp.where(seq > 0, mixed_halo[:, cols], jnp.zeros((TAPS, TILE), BF16))
        spec = mixed_spec[:, cols] + spectrum(pl.ds(0, TAPS), halo)
        mixed_spec[:, cols] = spec
        real, imag = spec[:HALF], spec[HALF:]
        tap_real, tap_imag = tap_spec[pl.ds(0, HALF), cols], tap_spec[pl.ds(HALF, HALF), cols]
        value_now = restore(
            pl.ds(0, ROWS),
            real * tap_real - imag * tap_imag,
            real * tap_imag + imag * tap_real,
        )
        state[:, cols] = value_now
        gated[pl.ds(0, ROWS), cols] = (query[:, cols].astype(F32) * value_now).astype(BF16)

    gated_sent = send(gated.at[pl.ds(0, ROWS)], gated.at[pl.ds(ROWS, ROWS)], to_core)

    right_top.wait_recv()
    forward_right = pass_cot(left, top, to_right)
    left_bottom.wait_recv()
    forward_left = pass_cot(right, bottom, to_left)

    near_copies, side_copies, corner_copies, core_copies = [], [], [], []
    here, beside = weight_rows(y[0], odd, core), weight_rows(1 - y[0], odd, core)
    above, corner = weight_rows(y[0], 1 - odd, core), weight_rows(1 - y[0], 1 - odd, core)

    def weight_spot(rows, number):
        part = pl.ds(pl.multiple_of(rows.start + number % 2 * 64, 64), 64)
        return full_weight.at[(1 - dp) * 2 + number // 2, part]

    def share_import(number):
        imports[number].wait_recv()
        spot = weight_spot(here, number)
        near_copies.append(send(spot, spot, to_near))
        side_copies.append(send(spot, spot, to_side[number % 2]))
        core_copies.append(send(spot, spot, to_core))

    def share_near(number):
        near_copies[number].wait_recv()
        spot = weight_spot(beside, number)
        corner_copies.append(send(spot, spot, to_side[number % 2]))
        core_copies.append(send(spot, spot, to_core))

    def share_last(copy, rows, number):
        copy.wait_recv()
        spot = weight_spot(rows, number)
        core_copies.append(send(spot, spot, to_core))

    first = [[] for _ in range(4)]

    def first_view(ref, quarter, slot):
        if quarter < 2:
            return ref.at[quarter, slot[0], slot[1], slot[2]]
        return ref.at[quarter, slot[0], slot[1]]

    def first_landing(quarter, chunk, i):
        return landing[quarter * 5].at[chunk] if quarter < 2 else landing[quarter * 5].at[chunk, i]

    first_targets = [to_near, to_far, to_side[0], to_side[1]]

    def products(chunk, owner):
        low, group = lax.div(owner, 2), pl.ds(lax.rem(owner, 2) * 4, 4)

        @pl.loop(0, 4)
        def _(quarter):
            rows = turned[pl.ds(owner * 4, 4)].reshape(512, 2 * ROWS)
            block = matmul(rows, gated[:, columns(quarter)]).astype(BF16)
            partial[quarter, low, group] = block.reshape(4, 2, 64, TILE)

    def halve(chunk, owner, quarters):
        for quarter in quarters:
            for i, slot in enumerate(first_slots(quarter, owner, y, z, False)):
                first[quarter].append(
                    send(
                        first_view(partial, quarter, slot),
                        first_landing(quarter, chunk, i),
                        first_targets[quarter],
                    )
                )

    share_import(0)
    share_import(1)
    turned_own.wait_recv()
    gated_sent.wait_recv()
    products(0, tp)
    halve(0, tp, (1,))
    share_import(2)
    share_import(3)
    share_near(0)
    share_near(1)
    right_bottom.wait_recv()
    turned_left = turn(left)
    left_top.wait_recv()
    turned_right = turn(right)
    turned_left.wait_recv()
    products(1, left)
    halve(1, left, (1,))
    share_near(2)
    share_near(3)
    halve(0, tp, (0, 2, 3))
    halve(1, left, (0, 2, 3))
    turned_right.wait_recv()
    products(2, right)
    halve(2, right, (0, 1, 2, 3))
    forward_right.wait_recv()
    forward_left.wait_recv()
    turned_across = turn(across)
    for copy in own:
        copy.wait()

    @pl.loop(0, CHANNELS // TILE)
    def _(tile):
        cols = columns(tile)
        total = matmul_nt(full_cot[dp * 2], full_weight[dp * 2, cols])
        grad_gated[:, cols] = total + matmul_nt(full_cot[dp * 2 + 1], full_weight[dp * 2 + 1, cols])

    turned_across.wait_recv()
    products(3, across)
    halve(3, across, (0, 1, 2, 3))
    for number in range(4):
        share_last(side_copies[number], above, number)
    for number in range(4):
        share_last(corner_copies[number], corner, number)
    for copy in core_copies:
        copy.wait_recv()

    @pl.loop(0, CHANNELS // TILE)
    def _(tile):
        cols = columns(tile)
        total = grad_gated[:, cols]
        for i in range(2):
            owner = (1 - dp) * 2 + i
            total = total + matmul_nt(full_cot[owner], full_weight[owner, cols])
        made_query[:, cols] = (total * state[:, cols]).astype(BF16)
        signal[:, cols] = (total * query[:, cols].astype(F32)).astype(BF16)

    signal_sent = send(signal.at[top], signal_halo, to_prior)
    outgoing = [fetch(made_query, query_out)]

    @pl.loop(0, CHANNELS // TILE)
    def _(tile):
        cols = columns(tile)
        spec = spectrum(pl.ds(0, ROWS), signal[:, cols])
        signal_spec[:, cols] = spec
        real, imag = spec[:HALF], spec[HALF:]
        part_real, part_imag = mixed_spec[pl.ds(0, HALF), cols], mixed_spec[pl.ds(HALF, HALF), cols]
        lags = restore(
            pl.ds(2 * ROWS, TAPS),
            real * part_real + imag * part_imag,
            imag * part_real - real * part_imag,
        )
        for i in range(TILE // 128):
            block = lags[:, i * 128 : (i + 1) * 128].T
            lag_sum[tile * (TILE // 128) + i] = block.astype(BF16)

    copies = [
        send(lag_sum.at[members[i]], near_land.at[i - 1], to_member(members[i])) for i in range(1, 8)
    ]

    rounds = [None] * 4

    def exchange(quarter, step):
        axis, move = PLANS[quarter][step]
        there_y = move(y) if axis == "y" else y
        there_z = move(z) if axis == "z" else z
        landed = landing[quarter * 5 + step]
        rounds[quarter] = [
            send(slot_view(partial, quarter, slot), landed.at[i], place(there_y, there_z, core))
            for i, slot in enumerate(slots(PLANS[quarter], step, there_y, there_z))
        ]

    def combine(quarter, step):
        if step == 0:
            for copy in first[quarter]:
                copy.wait_recv()
            pairs = [
                (first_view(partial, quarter, slot), first_landing(quarter, chunk, i))
                for chunk, owner in enumerate((tp, left, right, across))
                for i, slot in enumerate(first_slots(quarter, owner, y, z, True))
            ]
        else:
            for copy in rounds[quarter]:
                copy.wait_recv()
            landed = landing[quarter * 5 + step]
            pairs = [
                (slot_view(partial, quarter, slot), landed.at[i])
                for i, slot in enumerate(slots(PLANS[quarter], step, y, z))
            ]
        for view, landed in pairs:
            total = view[...].astype(F32) + landed[...].astype(F32)
            if step < 4:
                view[...] = total.astype(BF16)
            else:
                made_weight[:, pl.ds(quarter * TILE, TILE)] = total * scale
        if step < 4:
            exchange(quarter, step + 1)

    for quarter in range(4):
        combine(quarter, 0)

    signal_sent.wait_recv()

    @pl.loop(0, CHANNELS // TILE)
    def _(tile):
        cols = columns(tile)
        halo = jnp.where(seq < 31, signal_halo[:, cols], jnp.zeros((TAPS, TILE), BF16))
        spec = signal_spec[:, cols] + spectrum(pl.ds(ROWS, TAPS), halo)
        real, imag = spec[:HALF], spec[HALF:]
        tap_real, tap_imag = tap_spec[pl.ds(0, HALF), cols], tap_spec[pl.ds(HALF, HALF), cols]
        back = restore(
            pl.ds(ROWS, ROWS),
            real * tap_real + imag * tap_imag,
            imag * tap_real - real * tap_imag,
        )
        made_key[:, cols] = (back * value[:, cols].astype(F32)).astype(BF16)
        made_value[:, cols] = (back * key[:, cols].astype(F32)).astype(BF16)

    outgoing += [fetch(made_key, key_out), fetch(made_value, value_out)]

    for copy in copies:
        copy.wait_recv()
    total = lag_sum[member].astype(F32)
    for i in range(7):
        total = total + near_land[i].astype(F32)
    lag_mid[...] = total.reshape(8, 16, TAPS)
    copies = [
        send(lag_mid.at[heights[i]], far_land.at[i - 1], place(y, heights[i], core))
        for i in range(1, 8)
    ]
    for quarter in range(4):
        combine(quarter, 1)
    for copy in copies:
        copy.wait_recv()
    total = lag_mid[z]
    for i in range(7):
        total = total + far_land[i]
    lag_out[member, z] = (total * scale).astype(BF16)
    mine = lag_out.at[member, z]
    copies = [send(mine, mine, place(y, heights[i], core)) for i in range(1, 8)]
    for quarter in range(4):
        combine(quarter, 2)
    for copy in copies:
        copy.wait_recv()
    mine = lag_out.at[member]
    copies = [send(mine, mine, to_member(members[i])) for i in range(1, 8)]
    for quarter in range(4):
        combine(quarter, 3)
    for copy in copies:
        copy.wait_recv()
    made_filter[...] = lag_out[...].astype(F32)
    outgoing.append(fetch(made_filter, filter_out))
    diagonal = lax.broadcasted_iota(jnp.int32, (128, 128), 0) == lax.broadcasted_iota(
        jnp.int32, (128, 128), 1
    )
    for i in range(8):
        first_lag = made_filter[i].reshape(128, TAPS)[:, 0:1]
        spread = jnp.where(diagonal, jnp.broadcast_to(first_lag, (128, 128)), 0.0)
        made_skip[pl.ds(i, 1)] = jnp.sum(spread, axis=0, keepdims=True)
    outgoing.append(fetch(made_skip, skip_out))
    for quarter in range(4):
        combine(quarter, 4)
    outgoing.append(fetch(made_weight, weight_out))
    for copy in started:
        copy.wait_send()
    for copy in outgoing:
        copy.wait()


def hand_on(*refs):
    count = (len(refs) - 2) // 3
    sources, targets, held = refs[:count], refs[count : 2 * count], refs[2 * count : 3 * count]
    in_sem, out_sem = refs[-2:]
    loads = [pltpu.make_async_copy(sources[i], held[i], in_sem.at[i]) for i in range(count)]
    stores = [pltpu.make_async_copy(held[i], targets[i], out_sem.at[i]) for i in range(count)]
    for copy in loads:
        copy.start()
    for load, store in zip(loads, stores):
        load.wait()
        store.start()
    for copy in stores:
        copy.wait()


def per_device(query_gate, key_gate, value_input, filter_taps, skip_gain, out_weight, cotangent):
    ahead, behind = spectrum_tables()
    anywhere = pl.BlockSpec(memory_space=pl.ANY)
    block = ((ROWS, CHANNELS), BF16)
    scratch = [
        block,
        block,
        block,
        ((CHANNELS, TAPS), BF16),
        ((1, CHANNELS), F32),
        (ahead.shape, BF16),
        (behind.shape, BF16),
        ((4, ROWS, 1024), BF16),
        ((4, CHANNELS, 1024), BF16),
        ((16, 128, 2 * ROWS), BF16),
        ((16, 128, ROWS), BF16),
        ((2 * ROWS, CHANNELS), BF16),
        block,
        ((TAPS, CHANNELS), BF16),
        block,
        ((TAPS, CHANNELS), BF16),
        ((SIZE, CHANNELS), F32),
        ((SIZE, CHANNELS), F32),
        ((SIZE, CHANNELS), F32),
        ((ROWS, CHANNELS), F32),
        ((ROWS, CHANNELS), F32),
        ((4, 2, 8, 2, 64, TILE), BF16),
        ((8, 128, TAPS), BF16),
        ((8, 8, 16, TAPS), BF16),
        ((7, 128, TAPS), BF16),
        ((8, 16, TAPS), F32),
        ((7, 16, TAPS), F32),
        ((8, 128), F32),
        block,
        block,
        block,
        ((8, 8, 16, TAPS), F32),
        ((8, 128), F32),
        ((64, CHANNELS), F32),
    ]
    results = pl.pallas_call(
        kernel,
        out_shape=(
            jax.ShapeDtypeStruct((ROWS, CHANNELS), BF16),
            jax.ShapeDtypeStruct((ROWS, CHANNELS), BF16),
            jax.ShapeDtypeStruct((ROWS, CHANNELS), BF16),
            jax.ShapeDtypeStruct((8, 8, 16, TAPS), F32),
            jax.ShapeDtypeStruct((8, 128), F32),
            jax.ShapeDtypeStruct((64, CHANNELS), F32),
        ),
        in_specs=[anywhere] * 9,
        out_specs=[anywhere] * 6,
        scratch_shapes=[pltpu.VMEM(shape, dtype) for shape, dtype in scratch]
        + [
            pltpu.SemaphoreType.DMA((COPIES,)),
            pltpu.SemaphoreType.DMA((COPIES,)),
            pltpu.SemaphoreType.DMA((16,)),
        ]
        + [pltpu.VMEM(shape, BF16) for shape in landing_shapes()],
        compiler_params=pltpu.CompilerParams(
            collective_id=0, has_side_effects=True, vmem_limit_bytes=56 * 1024 * 1024
        ),
    )(
        query_gate[0], key_gate[0], value_input[0], filter_taps, skip_gain[None, :],
        out_weight, cotangent[0], jnp.asarray(ahead), jnp.asarray(behind),
    )
    results = [
        results[0][None],
        results[1][None],
        results[2][None],
        results[3].reshape(CHANNELS, TAPS),
        results[4].reshape(CHANNELS),
        results[5],
    ]
    return tuple(
        pl.pallas_call(
            hand_on,
            out_shape=[jax.ShapeDtypeStruct(x.shape, x.dtype) for x in results],
            in_specs=[anywhere] * 6,
            out_specs=[anywhere] * 6,
            scratch_shapes=[pltpu.VMEM(x.shape, x.dtype) for x in results]
            + [pltpu.SemaphoreType.DMA((6,))] * 2,
        )(*results)
    )


def solution(mesh):
    return jax.shard_map(
        per_device,
        mesh=mesh,
        in_specs=(
            P("dp", "seq", "tp"),
            P("dp", "seq", "tp"),
            P("dp", "seq", "tp"),
            P("tp", None),
            P("tp"),
            P("tp", "dp"),
            P("dp", "seq", "tp"),
        ),
        out_specs=(
            P("dp", "seq", "tp"),
            P("dp", "seq", "tp"),
            P("dp", "seq", "tp"),
            P("tp", None),
            P("tp"),
            P(("seq", "dp"), "tp"),
        ),
        check_vma=False,
    )
```

time: 104 us -> 75.5 us (0.73)
  Pallas kernels: 93.4 us -> 74.8 us
  local copies, waits for them, and re-layouts: 10.1 us -> 0 us
    pallas_call x1, Pallas kernels: 93.4 us -> 72.2 us  [per_device(): pl.pallas_call(kernel, out_shape=(jax.ShapeDtypeStruct((ROWS, CHANNELS),...]
    unnamed x7 -> x0, local copies, waits for them, and re-layouts: 8.18 us -> none
    pallas_call x0 -> x1, Pallas kernels: none -> 2.54 us  [per_device(): pl.pallas_call(hand_on, out_shape=[jax.ShapeDtypeStruct(x.shape, x.dtype)...]
    slice x1 -> x0, local copies, waits for them, and re-layouts: 1.89 us -> none  [per_device(): grad_filter[:, 0]]
where the time goes in v2:
time: 75.5 us; the launch traced here: 75.4 us
  Pallas kernels  74.8 us (99%)
    pallas_call x1, Pallas kernels, per_device(): pl.pallas_call(kernel, out_shape=(jax.ShapeDtypeStruct((ROWS, CHANNELS),...  72.2 us
    pallas_call x1, Pallas kernels, per_device(): pl.pallas_call(hand_on, out_shape=[jax.ShapeDtypeStruct(x.shape, x.dtype)...  2.54 us

profile of v2, /device:TPU:1, one launch (start us, length us, event | category | flops | bytes accessed | tf_op | source)
XLA Modules:
  0.0 75.4 jit_solution(9294764045281211365)
XLA Ops:
  0.6 72.2 %shard_map.136 = (bf16[256,1024]{1,0:T(8,128)(2,1)}, bf16[256,1024]{1,0:T(8,128)(2,1)}, bf16[256,1024]{1,0:T(8,128)(2,1)}, f32[8,8,16,128]{3,2,1,0:T(8,128)}, f32[8,128]{1,0:T(8,128)}, /*index=5*/f32[64,1024]{1,0:T(8,128)}) custom-call(bf16[256,1024]{1,0:T(8,128)(2,1)} %bitcast.10, bf16[256,1024]{1,0:T(8,128)(2,1)} %bitcast.11, bf16[256,1024]{1,0:T(8,128)(2,1)} %bitcast.12, ...), custom_call_target="tpu_custom_call" | custom-call | tf_op jit(solution)/shard_map/pallas_call | solution.py:613
  72.9 2.5 %shard_map.137 = (bf16[1,256,1024]{2,1,0:T(8,128)(2,1)}, bf16[1,256,1024]{2,1,0:T(8,128)(2,1)}, bf16[1,256,1024]{2,1,0:T(8,128)(2,1)}, f32[1024,128]{1,0:T(8,128)}, f32[1024]{0:T(1024)}, /*index=5*/f32[64,1024]{1,0:T(8,128)}) custom-call(bf16[1,256,1024]{2,1,0:T(8,128)(2,1)} %bitcast.14, bf16[1,256,1024]{2,1,0:T(8,128)(2,1)} %bitcast.15, ...), custom_call_target="tpu_custom_call" | custom-call | tf_op jit(solution)/shard_map/pallas_call | solution.py:648

commit v3 on v2

v3 whole, which is shorter than its diff:
```python
import itertools
import math

import jax
import jax.numpy as jnp
import ml_dtypes
import numpy as np
from jax import lax
from jax.experimental import pallas as pl
from jax.experimental.pallas import tpu as pltpu
from jax.sharding import PartitionSpec as P

ROWS = 256
TAPS = 128
SIZE = ROWS + TAPS
HALF = SIZE // 2
CHANNELS = 1024
TILE = 256
STREAMS = 2
LANES = TILE // STREAMS
PER_QUARTER = 5 * STREAMS
SENT_ROWS = 2048
OUT_EXTRA, OUT_SETS = 4, 3
COPIES = 94
BF16 = jnp.bfloat16
F32 = jnp.float32


PARTS = ((TAPS, ROWS), (0, TAPS), (0, ROWS), (ROWS, TAPS))
LATE_BLOCK, EARLY_HALO, EARLY_BLOCK, LATE_HALO = 0, 2 * ROWS, 2 * SIZE, 2 * SIZE + 2 * ROWS


def split_table(table):
    high = table.astype(ml_dtypes.bfloat16)
    return high, (table - high.astype(np.float64)).astype(ml_dtypes.bfloat16)


def spectrum_tables():
    odd = 2 * np.arange(HALF) + 1

    def angles(positions):
        return np.pi * ((odd[:, None] * positions[None, :]) % (2 * SIZE)) / SIZE

    ahead = angles(np.arange(SIZE))
    forward = np.concatenate([np.cos(ahead), -np.sin(ahead)], axis=0)
    places = np.concatenate(
        [np.arange(TAPS, SIZE), np.arange(ROWS), np.arange(-TAPS, 0)]
    )
    behind = angles(places).T
    inverse = (2.0 / SIZE) * np.concatenate([np.cos(behind), -np.sin(behind)], axis=1)
    high, low = split_table(forward)
    pieces = [piece[:, start : start + size] for start, size in PARTS for piece in (high, low)]
    back_high, back_low = split_table(inverse)
    return (
        np.concatenate(pieces, axis=1),
        np.concatenate([back_high, back_low, back_high], axis=1),
    )


def matmul(left, right):
    return jnp.dot(left, right, preferred_element_type=F32)


def matmul_nt(left, right):
    return lax.dot_general(
        left, right, (((1,), (1,)), ((), ())), preferred_element_type=F32
    )


def y_near(y):
    return (1 - y[0], y[1])


def y_far(y):
    return (1 - y[0], 1 - y[1])


def z_up(z):
    return z + 1 - 2 * lax.rem(z, 2)


def z_down(z):
    return lax.rem(z + 2 * lax.rem(z, 2) + 7, 8)


def z_three(z):
    return lax.rem(z + 11 - 6 * lax.rem(z, 2), 8)


def z_back_three(z):
    return lax.rem(z + 5 + 6 * lax.rem(z, 2), 8)


PLANS = (
    (("y", y_near), ("y", y_far), ("z", z_up), ("z", z_down), ("z", z_three)),
    (("y", y_far), ("y", y_near), ("z", z_down), ("z", z_up), ("z", z_back_three)),
    (("z", z_up), ("z", z_down), ("y", y_near), ("y", y_far), ("z", z_three)),
    (("z", z_down), ("z", z_up), ("y", y_far), ("y", y_near), ("z", z_back_three)),
)


def kept(rest, place):
    if not rest:
        return [place]
    return kept(rest[1:], place) + kept(rest[1:], rest[0](place))


def remaining(plan, step, axis):
    return [move for name, move in plan[step + 1 :] if name == axis]


def slots(plan, step, y, z):
    y_rest, z_rest = remaining(plan, step, "y"), remaining(plan, step, "z")
    y_list = [None] if len(y_rest) == 2 else kept(y_rest, y)
    z_list = [None] if len(z_rest) == 3 else kept(z_rest, z)
    return [(one, other) for one in y_list for other in z_list]


def slot_view(ref, quarter, slot, lanes):
    y, z = slot
    if y is None:
        return ref.at[quarter, :, z, :, :, lanes]
    if z is None:
        return ref.at[quarter, y[0], :, y[1], :, lanes]
    return ref.at[quarter, y[0], z, y[1], :, lanes]


def planes_of(size):
    for planes in range(1, 5):
        if size % (2048 * 16 * planes) == 0 and size // (2048 * planes) <= 1024:
            return planes
    return None


def landing_shapes():
    shapes = []
    for plan in PLANS:
        shapes += [(4, 4, 64, LANES) if plan[0][0] == "y" else (4, 2, 2, 64, LANES)] * STREAMS
        for step in range(1, 5):
            y_rest, z_rest = remaining(plan, step, "y"), remaining(plan, step, "z")
            if len(y_rest) == 2:
                shape = (2 ** len(z_rest), 2, 2, 64, LANES)
            elif len(z_rest) == 3:
                shape = (2 ** len(y_rest), 8, 64, LANES)
            else:
                shape = (2 ** (len(y_rest) + len(z_rest)), 64, LANES)
            shapes += [shape] * STREAMS
    return shapes


def first_slots(quarter, owner, y, z, keep):
    low, half = lax.div(owner, 2), lax.rem(owner, 2)
    group = pl.ds(half * 4, 4)
    other = 0 if keep else 1
    if quarter == 0:
        return [(low, group, lax.rem(y[1] + y[0] + low + other, 2))]
    if quarter == 1:
        return [(low, group, lax.rem(y[1] + other, 2))]
    if quarter == 2:
        kind = lax.rem(lax.div(lax.rem(z, 4) + 1, 2) + other, 2)
        return [(low, half * 4 + kind + i * (3 - 2 * kind)) for i in range(2)]
    kind = lax.rem(lax.div(lax.rem(z, 4), 2) + other, 2)
    return [(low, half * 4 + kind * 2 + i) for i in range(2)]


def kernel(
    query_in, key_in, value_in, taps_in, skip_in, weight, cot, ahead_in, behind_in,
    made_query, made_key, made_value, made_filter, made_skip, made_weight,
    query, key, value, taps, skip, ahead, behind,
    full_cot, full_weight, turned, turned_away, gated, mixed, mixed_halo, signal, signal_halo,
    tap_spec, mixed_spec, signal_spec, state, grad_gated, partial, lag_sum, lag_out,
    near_land, lag_mid, far_land, send_sem, recv_sem, local_sem, *landing,
):
    seq, tp, dp = lax.axis_index("seq"), lax.axis_index("tp"), lax.axis_index("dp")
    core = lax.rem(seq, 2)
    z = lax.rem(lax.div(seq, 2), 8)
    y = (lax.div(seq, 16), dp)
    scale = 1.0 / math.sqrt(2 * 32 * ROWS)

    def place(y, z, core):
        return ((y[0] * 8 + z) * 2 + core, tp, y[1])

    right, left, across = lax.rem(tp + 1, 4), lax.rem(tp + 3, 4), lax.rem(tp + 2, 4)
    to_right, to_left = (seq, right, dp), (seq, left, dp)
    to_next, to_prior = (lax.rem(seq + 1, 32), tp, dp), (lax.rem(seq + 31, 32), tp, dp)
    to_core = place(y, z, 1 - core)
    to_near, to_far = place(y_near(y), z, core), place(y_far(y), z, core)
    to_side = [place(y, z_up(z), core), place(y, z_down(z), core)]
    member = (y[1] * 2 + y[0]) * 2 + core

    def to_member(index):
        high = lax.div(index, 4)
        return place((lax.rem(lax.div(index, 2), 2), high), z, lax.rem(index, 2))

    members = [lax.rem(member + i, 8) for i in range(8)]
    heights = [lax.rem(z + i, 8) for i in range(8)]

    barrier = pltpu.get_barrier_semaphore()
    greeted = [to_right, to_left, to_next, to_prior]
    greeted += [to_member(members[i]) for i in range(1, 8)]
    greeted += [place(y, heights[i], core) for i in range(1, 8)]
    for target in greeted:
        pl.semaphore_signal(
            barrier, inc=1, device_id=target, device_id_type=pl.DeviceIdType.MESH
        )

    local_numbers = itertools.count()

    def fetch(source, target):
        copy = pltpu.make_async_copy(source, target, local_sem.at[next(local_numbers)])
        copy.start()
        return copy

    key_copy, value_copy = fetch(key_in, key), fetch(value_in, value)
    cot_copy = fetch(cot, full_cot.at[tp])
    table_copies = [fetch(ahead_in, ahead), fetch(taps_in, taps), fetch(skip_in, skip)]
    state_copies = [fetch(behind_in, behind), fetch(query_in, query)]
    pl.semaphore_wait(barrier, len(greeted))

    numbers = itertools.count()
    started = []

    def describe(source, target_ref, target, number, out_number):
        return pltpu.make_async_remote_copy(
            src_ref=source,
            dst_ref=target_ref,
            send_sem=send_sem.at[out_number],
            recv_sem=recv_sem.at[number],
            device_id=target,
            device_id_type=pl.DeviceIdType.MESH,
        )

    def send(source, target_ref, target, group=None, out=None):
        size = math.prod(source.shape) * source.dtype.itemsize
        if out is None:
            if not started or started[-1] >= SENT_ROWS * 2048 and planes_of(started[-1]):
                started.append(0)
            started[-1] += size
        number = next(numbers) if group is None else group[1]
        out_number = OUT_EXTRA + len(started) - 1 if out is None else out
        copy = describe(source, target_ref, target, number, out_number)
        copy.start()
        return copy

    def gather(landed):
        number = next(numbers)
        return describe(landed, landed, to_core, number, 0), number

    top, bottom = pl.ds(0, 128), pl.ds(128, 128)

    def pass_cot(owner, part, target):
        spot = full_cot.at[owner, part]
        return send(spot, spot, target)

    right_top = send(cot.at[top], full_cot.at[tp, top], to_right)
    left_bottom = send(cot.at[bottom], full_cot.at[tp, bottom], to_left)

    def weight_rows(low, odd, core):
        return pl.ds(pl.multiple_of(((low * 2 + odd) * 2 + core) * 128, 128), 128)

    odd = lax.rem(z, 2)
    given = weight_rows(1 - y[0], odd, core)
    imports = []
    for i in range(2):
        for r in range(4):
            rows = pl.ds(pl.multiple_of(given.start + r * 32, 32), 32)
            source = weight.at[rows, pl.ds(i * 1024, 1024)]
            imports.append(send(source, full_weight.at[dp * 2 + i, rows], to_far))
    right_bottom = send(cot.at[bottom], full_cot.at[tp, bottom], to_right)
    left_top = send(cot.at[top], full_cot.at[tp, top], to_left)
    own = [fetch(weight.at[:, pl.ds(i * 1024, 1024)], full_weight.at[dp * 2 + i]) for i in range(2)]

    key_copy.wait()
    value_copy.wait()
    mixed[...] = (key[...].astype(F32) * value[...].astype(F32)).astype(BF16)
    mixed_sent = send(mixed.at[bottom], mixed_halo, to_next)

    def turn(owner, start, size):
        tokens, far_tokens = pl.ds(start, size), pl.ds(ROWS + start, size)
        for i in range(4):
            mine = pl.ds(pl.multiple_of((i * 2 + core) * 128, 128), 128)
            other = pl.ds(pl.multiple_of((i * 2 + 1 - core) * 128, 128), 128)
            turned[owner * 4 + i, :, tokens] = full_cot[owner, tokens, mine].T
            turned_away[owner * 4 + i, :, tokens] = full_cot[owner, tokens, other].T
        group = pl.ds(owner * 4, 4)
        return send(turned_away.at[group, :, tokens], turned.at[group, :, far_tokens], to_core)

    cot_copy.wait()
    turned_own = turn(tp, 0, ROWS)

    def columns(tile):
        return pl.ds(pl.multiple_of(tile * TILE, TILE), TILE)

    def spectrum(start, block):
        table = ahead[:, pl.ds(start, 2 * block.shape[0])]
        return matmul(table, jnp.concatenate([block, block], axis=0))

    def restore(places, real, imag):
        spec = jnp.concatenate([real, imag], axis=0)
        high = spec.astype(BF16)
        low = (spec - high.astype(F32)).astype(BF16)
        return matmul(behind[places], jnp.concatenate([high, high, low], axis=0))

    for copy in table_copies:
        copy.wait()

    @pl.loop(0, CHANNELS // TILE)
    def _(tile):
        cols = columns(tile)
        block = taps[cols]
        table = ahead[:, pl.ds(EARLY_HALO, 2 * TAPS)]
        spec = matmul_nt(table, jnp.concatenate([block, block], axis=1))
        tap_spec[pl.ds(0, HALF), cols] = spec[:HALF] + skip[:, cols]
        tap_spec[pl.ds(HALF, HALF), cols] = spec[HALF:]
        mixed_spec[:, cols] = spectrum(LATE_BLOCK, mixed[:, cols])

    def block_rows(kind, core):
        low = y[0] if kind in ("here", "above") else 1 - y[0]
        return weight_rows(low, odd if kind in ("here", "beside") else 1 - odd, core)

    kinds = ("here", "beside", "above", "corner")
    others = pl.ds((1 - dp) * 2, 2)
    from_core = {kind: gather(full_weight.at[others, block_rows(kind, 1 - core)]) for kind in kinds}
    from_side = gather(full_weight.at[others, block_rows("above", core)])
    from_corner = [
        gather(full_weight.at[(1 - dp) * 2 + i, block_rows("corner", core)]) for i in range(2)
    ]
    near_copies = []

    def weight_spot(kind, number):
        part = pl.ds(pl.multiple_of(block_rows(kind, core).start + number % 4 * 32, 32), 32)
        return full_weight.at[(1 - dp) * 2 + number // 4, part]

    def share_core(kind, i):
        spot = full_weight.at[(1 - dp) * 2 + i, block_rows(kind, core)]
        send(spot, spot, to_core, from_core[kind])

    def share_import(number):
        imports[number].wait_recv()
        spot = weight_spot("here", number)
        near_copies.append(send(spot, spot, to_near))
        send(spot, spot, to_side[number % 2], from_side)
        if number % 4 == 3:
            share_core("here", number // 4)

    def share_near(number):
        near_copies[number].wait_recv()
        spot = weight_spot("beside", number)
        send(spot, spot, to_side[number % 2], from_corner[number // 4])
        if number % 4 == 3:
            share_core("beside", number // 4)

    def convolve(start):
        @pl.loop(start, start + 2)
        def _(tile):
            cols = columns(tile)
            halo = jnp.where(seq > 0, mixed_halo[:, cols], jnp.zeros((TAPS, TILE), BF16))
            spec = mixed_spec[:, cols] + spectrum(EARLY_HALO, halo)
            mixed_spec[:, cols] = spec
            real, imag = spec[:HALF], spec[HALF:]
            tap_real, tap_imag = tap_spec[pl.ds(0, HALF), cols], tap_spec[pl.ds(HALF, HALF), cols]
            value_now = restore(
                pl.ds(0, ROWS),
                real * tap_real - imag * tap_imag,
                real * tap_imag + imag * tap_real,
            )
            state[:, cols] = value_now
            gated[pl.ds(0, ROWS), cols] = (query[:, cols].astype(F32) * value_now).astype(BF16)

    for copy in state_copies:
        copy.wait()
    mixed_sent.wait_recv()

    share_import(0)
    convolve(0)
    share_import(1)
    convolve(2)
    gated_sent = send(gated.at[pl.ds(0, ROWS)], gated.at[pl.ds(ROWS, ROWS)], to_core)

    first = [
        [gather(landing[quarter * PER_QUARTER + stream]) for stream in range(STREAMS)]
        for quarter in range(4)
    ]

    def lanes_of(stream):
        return pl.ds(stream * LANES, LANES)

    def first_view(quarter, slot, stream):
        if quarter < 2:
            return partial.at[quarter, slot[0], slot[1], slot[2], :, lanes_of(stream)]
        return partial.at[quarter, slot[0], slot[1], :, :, lanes_of(stream)]

    def first_landing(quarter, chunk, i, stream):
        landed = landing[quarter * PER_QUARTER + stream]
        return landed.at[chunk] if quarter < 2 else landed.at[chunk, i]

    first_targets = [to_near, to_far, to_side[0], to_side[1]]

    def products(chunk, owner):
        low, group = lax.div(owner, 2), pl.ds(lax.rem(owner, 2) * 4, 4)

        @pl.loop(0, 4)
        def _(quarter):
            rows = turned[pl.ds(owner * 4, 4)].reshape(512, 2 * ROWS)
            block = matmul(rows, gated[:, columns(quarter)]).astype(BF16)
            partial[quarter, low, group] = block.reshape(4, 2, 64, TILE)

    def halve(chunk, owner, stream):
        for quarter in range(4):
            for i, slot in enumerate(first_slots(quarter, owner, y, z, False)):
                send(
                    first_view(quarter, slot, stream),
                    first_landing(quarter, chunk, i, stream),
                    first_targets[quarter],
                    first[quarter][stream],
                )

    share_import(2)
    right_top.wait_recv()
    forward_right = pass_cot(left, top, to_right)
    left_bottom.wait_recv()
    forward_left = pass_cot(right, bottom, to_left)
    turned_left = [turn(left, 0, 128)]
    turned_right = [turn(right, 128, 128)]
    share_import(3)
    share_near(0)
    turned_own.wait_recv()
    gated_sent.wait_recv()
    products(0, tp)
    halve(0, tp, 0)
    share_import(4)
    share_near(1)
    share_import(5)
    share_near(2)
    share_import(6)
    share_near(3)
    right_bottom.wait_recv()
    turned_left.append(turn(left, 128, 128))
    left_top.wait_recv()
    turned_right.append(turn(right, 0, 128))
    for copy in own:
        copy.wait()
    late = jnp.where(lax.div(across, 2) == dp, across, dp * 4 + 1 - tp)
    early = dp * 4 + 1 - late

    @pl.loop(0, CHANNELS // TILE)
    def _(tile):
        cols = columns(tile)
        grad_gated[:, cols] = matmul_nt(full_cot[early], full_weight[early, cols])

    share_import(7)
    share_near(4)
    for copy in turned_left:
        copy.wait_recv()
    products(1, left)
    halve(1, left, 0)
    share_near(5)
    share_near(6)
    for copy in turned_right:
        copy.wait_recv()
    products(2, right)
    halve(2, right, 0)
    forward_right.wait_recv()
    forward_left.wait_recv()
    turned_across = turn(across, 0, ROWS)
    share_near(7)
    halve(0, tp, 1)
    halve(1, left, 1)
    @pl.loop(0, CHANNELS // TILE)
    def _(tile):
        cols = columns(tile)
        grad_gated[:, cols] += matmul_nt(full_cot[late], full_weight[late, cols])

    turned_across.wait_recv()
    products(3, across)
    halve(3, across, 0)
    halve(2, right, 1)
    halve(3, across, 1)

    from_side[0].wait_recv()
    share_core("above", 0)
    share_core("above", 1)
    from_corner[0][0].wait_recv()
    share_core("corner", 0)
    signal_sent = gather(signal_halo)

    def finish(tile, kind):
        from_core[kind][0].wait_recv()
        cols = columns(tile)
        total = grad_gated[:, cols]
        for i in range(2):
            owner = (1 - dp) * 2 + i
            total = total + matmul_nt(full_cot[owner], full_weight[owner, cols])
        made_query[:, cols] = (total * state[:, cols]).astype(BF16)
        signal[:, cols] = (total * query[:, cols].astype(F32)).astype(BF16)
        send(signal.at[top, cols], signal_halo.at[:, cols], to_prior, signal_sent)
        spec = spectrum(EARLY_BLOCK, signal[:, cols])
        signal_spec[:, cols] = spec
        real, imag = spec[:HALF], spec[HALF:]
        part_real, part_imag = mixed_spec[pl.ds(0, HALF), cols], mixed_spec[pl.ds(HALF, HALF), cols]
        lags = restore(
            pl.ds(2 * ROWS, TAPS),
            real * part_real + imag * part_imag,
            imag * part_real - real * part_imag,
        )
        for i in range(TILE // 128):
            block = lags[:, i * 128 : (i + 1) * 128].T
            lag_sum[tile * (TILE // 128) + i] = block.astype(BF16)

    rounds = {}

    def exchange(quarter, step, stream):
        axis, move = PLANS[quarter][step]
        there_y = move(y) if axis == "y" else y
        there_z = move(z) if axis == "z" else z
        landed = landing[quarter * PER_QUARTER + step * STREAMS + stream]
        group = gather(landed)
        for i, slot in enumerate(slots(PLANS[quarter], step, there_y, there_z)):
            view = slot_view(partial, quarter, slot, lanes_of(stream))
            send(view, landed.at[i], place(there_y, there_z, core), group)
        rounds[quarter, step, stream] = group[0], landed

    def combine(quarter, step, stream):
        lanes = lanes_of(stream)
        if step == 0:
            first[quarter][stream][0].wait_recv()
            pairs = [
                (first_view(quarter, slot, stream), first_landing(quarter, chunk, i, stream))
                for chunk, owner in enumerate((tp, left, right, across))
                for i, slot in enumerate(first_slots(quarter, owner, y, z, True))
            ]
        else:
            copy, landed = rounds[quarter, step, stream]
            copy.wait_recv()
            pairs = [
                (slot_view(partial, quarter, slot, lanes), landed.at[i])
                for i, slot in enumerate(slots(PLANS[quarter], step, y, z))
            ]
        for view, landed in pairs:
            total = view[...].astype(F32) + landed[...].astype(F32)
            if step < 4:
                view[...] = total.astype(BF16)
            else:
                place_out = pl.ds(quarter * TILE + stream * LANES, LANES)
                made_weight[:, place_out] = total * scale
        if step < 4:
            exchange(quarter, step + 1, stream)

    def combine_all(step, stream):
        for quarter in range(4):
            combine(quarter, step, stream)

    def restore_back(start):
        @pl.loop(start, start + 2)
        def _(tile):
            cols = columns(tile)
            halo = jnp.where(seq < 31, signal_halo[:, cols], jnp.zeros((TAPS, TILE), BF16))
            spec = signal_spec[:, cols] + spectrum(LATE_HALO, halo)
            real, imag = spec[:HALF], spec[HALF:]
            tap_real, tap_imag = tap_spec[pl.ds(0, HALF), cols], tap_spec[pl.ds(HALF, HALF), cols]
            back = restore(
                pl.ds(ROWS, ROWS),
                real * tap_real + imag * tap_imag,
                imag * tap_real - real * tap_imag,
            )
            made_key[:, cols] = (back * value[:, cols].astype(F32)).astype(BF16)
            made_value[:, cols] = (back * key[:, cols].astype(F32)).astype(BF16)

    finish(y[0] * 2 + odd, "here")
    finish((1 - y[0]) * 2 + odd, "beside")
    from_corner[1][0].wait_recv()
    share_core("corner", 1)
    finish(y[0] * 2 + 1 - odd, "above")
    finish((1 - y[0]) * 2 + 1 - odd, "corner")

    near_sums = gather(near_land)
    for i in range(1, 8):
        send(lag_sum.at[members[i]], near_land.at[i - 1], to_member(members[i]), near_sums, 0)

    combine_all(0, 0)
    combine_all(0, 1)
    near_sums[0].wait_recv()
    total = lag_sum[member].astype(F32)
    for i in range(7):
        total = total + near_land[i].astype(F32)
    lag_mid[...] = total.reshape(8, 16, TAPS)
    far_sums = gather(far_land)
    for i in range(1, 8):
        send(lag_mid.at[heights[i]], far_land.at[i - 1], place(y, heights[i], core), far_sums, 1)

    combine_all(1, 0)
    signal_sent[0].wait_recv()

    restore_back(0)
    combine_all(1, 1)
    combine_all(2, 0)
    far_sums[0].wait_recv()
    total = lag_mid[z]
    for i in range(7):
        total = total + far_land[i]
    lag_out[member, z] = (total * scale).astype(BF16)
    mine = lag_out.at[member, z]
    copies = [send(mine, mine, place(y, heights[i], core), None, 2) for i in range(1, 8)]
    restore_back(2)
    combine_all(2, 1)
    combine_all(3, 0)
    for copy in copies:
        copy.wait_recv()
    mine = lag_out.at[member]
    copies = [send(mine, mine, to_member(members[i]), None, 3) for i in range(1, 8)]
    combine_all(3, 1)
    combine_all(4, 0)
    for copy in copies:
        copy.wait_recv()
    made_filter[...] = lag_out[...].astype(F32)
    diagonal = lax.broadcasted_iota(jnp.int32, (128, 128), 0) == lax.broadcasted_iota(
        jnp.int32, (128, 128), 1
    )
    for i in range(8):
        first_lag = made_filter[i].reshape(128, TAPS)[:, 0:1]
        spread = jnp.where(diagonal, jnp.broadcast_to(first_lag, (128, 128)), 0.0)
        made_skip[pl.ds(i, 1)] = jnp.sum(spread, axis=0, keepdims=True)
    combine_all(4, 1)
    sent = [near_land, far_land, near_land.at[:, pl.ds(0, 16)], near_land]
    for size in started:
        planes = planes_of(size)
        sent.append(full_weight.at[pl.ds(0, planes), pl.ds(0, size // 2048 // planes)])
    for out_number, block in enumerate(sent):
        describe(block, block, to_core, 0, out_number).wait_send()


def hand_on(*refs):
    count = (len(refs) - 1) // 2
    copies = [
        pltpu.make_async_copy(refs[i], refs[count + i], refs[-1].at[i]) for i in range(count)
    ]
    for copy in copies:
        copy.start()
    for copy in copies:
        copy.wait()


def per_device(query_gate, key_gate, value_input, filter_taps, skip_gain, out_weight, cotangent):
    ahead, behind = spectrum_tables()
    anywhere = pl.BlockSpec(memory_space=pl.ANY)
    block = ((ROWS, CHANNELS), BF16)
    scratch = [
        block,
        block,
        block,
        ((CHANNELS, TAPS), BF16),
        ((1, CHANNELS), F32),
        (ahead.shape, BF16),
        (behind.shape, BF16),
        ((4, ROWS, 1024), BF16),
        ((4, CHANNELS, 1024), BF16),
        ((16, 128, 2 * ROWS), BF16),
        ((16, 128, ROWS), BF16),
        ((2 * ROWS, CHANNELS), BF16),
        block,
        ((TAPS, CHANNELS), BF16),
        block,
        ((TAPS, CHANNELS), BF16),
        ((SIZE, CHANNELS), F32),
        ((SIZE, CHANNELS), F32),
        ((SIZE, CHANNELS), F32),
        ((ROWS, CHANNELS), F32),
        ((ROWS, CHANNELS), F32),
        ((4, 2, 8, 2, 64, TILE), BF16),
        ((8, 128, TAPS), BF16),
        ((8, 8, 16, TAPS), BF16),
        ((7, 128, TAPS), BF16),
        ((8, 16, TAPS), F32),
        ((7, 16, TAPS), F32),
    ]
    results = pl.pallas_call(
        kernel,
        out_shape=[
            pltpu.VMEM((ROWS, CHANNELS), BF16),
            pltpu.VMEM((ROWS, CHANNELS), BF16),
            pltpu.VMEM((ROWS, CHANNELS), BF16),
            pltpu.VMEM((8, 8, 16, TAPS), F32),
            pltpu.VMEM((8, 128), F32),
            pltpu.VMEM((64, CHANNELS), F32),
        ],
        in_specs=[anywhere] * 9,
        out_specs=[pl.BlockSpec(memory_space=pltpu.VMEM)] * 6,
        scratch_shapes=[pltpu.VMEM(shape, dtype) for shape, dtype in scratch]
        + [
            pltpu.SemaphoreType.DMA((OUT_EXTRA + OUT_SETS,)),
            pltpu.SemaphoreType.DMA((COPIES,)),
            pltpu.SemaphoreType.DMA((10,)),
        ]
        + [pltpu.VMEM(shape, BF16) for shape in landing_shapes()],
        compiler_params=pltpu.CompilerParams(
            collective_id=0, has_side_effects=True, vmem_limit_bytes=56 * 1024 * 1024
        ),
    )(
        query_gate[0], key_gate[0], value_input[0], filter_taps, skip_gain[None, :],
        out_weight, cotangent[0], jnp.asarray(ahead), jnp.asarray(behind),
    )
    results = [
        results[0][None],
        results[1][None],
        results[2][None],
        results[3].reshape(CHANNELS, TAPS),
        results[4].reshape(CHANNELS),
        results[5],
    ]
    return tuple(
        pl.pallas_call(
            hand_on,
            out_shape=[jax.ShapeDtypeStruct(x.shape, x.dtype) for x in results],
            in_specs=[pl.BlockSpec(memory_space=pltpu.VMEM)] * 6,
            out_specs=[anywhere] * 6,
            scratch_shapes=[pltpu.SemaphoreType.DMA((6,))],
        )(*[pltpu.with_memory_space_constraint(x, pltpu.VMEM) for x in results])
    )


def solution(mesh):
    return jax.shard_map(
        per_device,
        mesh=mesh,
        in_specs=(
            P("dp", "seq", "tp"),
            P("dp", "seq", "tp"),
            P("dp", "seq", "tp"),
            P("tp", None),
            P("tp"),
            P("tp", "dp"),
            P("dp", "seq", "tp"),
        ),
        out_specs=(
            P("dp", "seq", "tp"),
            P("dp", "seq", "tp"),
            P("dp", "seq", "tp"),
            P("tp", None),
            P("tp"),
            P(("seq", "dp"), "tp"),
        ),
        check_vma=False,
    )
```

time: 75.5 us -> 68.5 us (0.907)
  Pallas kernels: 74.8 us -> 67.7 us
    pallas_call x1, Pallas kernels: 72.2 us -> 66.3 us  [per_device(): pl.pallas_call(kernel, out_shape=[pltpu.VMEM((ROWS, CHANNELS), BF16), plt...]
    pallas_call x1, Pallas kernels: 2.54 us -> 1.45 us  [per_device(): pl.pallas_call(hand_on, out_shape=[jax.ShapeDtypeStruct(x.shape, x.dtype)...]
where the time goes in v3:
time: 68.5 us; the launch traced here: 68.4 us
  Pallas kernels  67.7 us (99%)
    pallas_call x1, Pallas kernels, per_device(): pl.pallas_call(kernel, out_shape=[pltpu.VMEM((ROWS, CHANNELS), BF16), plt...  66.3 us
    pallas_call x1, Pallas kernels, per_device(): pl.pallas_call(hand_on, out_shape=[jax.ShapeDtypeStruct(x.shape, x.dtype)...  1.45 us

profile of v3, /device:TPU:1, one launch (start us, length us, event | category | flops | bytes accessed | tf_op | source)
XLA Modules:
  0.0 68.4 jit_solution(3838230976410808891)
XLA Ops:
  0.6 66.3 %shard_map.136 = (bf16[256,1024]{1,0:T(8,128)(2,1)S(1)}, bf16[256,1024]{1,0:T(8,128)(2,1)S(1)}, bf16[256,1024]{1,0:T(8,128)(2,1)S(1)}, f32[8,8,16,128]{3,2,1,0:T...) custom-call(bf16[256,1024]{1,0:T(8,128)(2,1)} %bitcast.15, bf16[256,1024]{1,0:T(8,128)(2,1)} %bitcast.16, ...), custom_call_target="tpu_custom_call" | custom-call | tf_op jit(solution)/shard_map/pallas_call | solution.py:676
  66.9 1.5 %shard_map.137 = (bf16[1,256,1024]{2,1,0:T(8,128)(2,1)}, bf16[1,256,1024]{2,1,0:T(8,128)(2,1)}, bf16[1,256,1024]{2,1,0:T(8,128)(2,1)}, f32[1024,128]{1,0:T(8,128)}, f32[1024]{0:T(1024)}, /*index=5*/f32[64,1024]{1,0:T(8,128)}) custom-call(bf16[1,256,1024]{2,1,0:T(8,128)(2,1)S(1)} %bitcast.10, bf16[1,256,1024]{2,1,0:T(8,128)(2,1)S(1)} %bitcast.11, ...), custom_call_target="tpu_custom_call" | custom-call | tf_op jit(solution)/shard_map/pallas_call | solution.py:711

commit v4 on v3

--- a/solution.py
+++ b/solution.py
@@ -21,7 +21,7 @@
 PER_QUARTER = 5 * STREAMS
 SENT_ROWS = 2048
 OUT_EXTRA, OUT_SETS = 4, 3
-COPIES = 94
+COPIES = 96
 BF16 = jnp.bfloat16
 F32 = jnp.float32
 
@@ -215,6 +215,9 @@
     cot_copy = fetch(cot, full_cot.at[tp])
     table_copies = [fetch(ahead_in, ahead), fetch(taps_in, taps), fetch(skip_in, skip)]
     state_copies = [fetch(behind_in, behind), fetch(query_in, query)]
+    key_copy.wait()
+    value_copy.wait()
+    mixed[...] = (key[...].astype(F32) * value[...].astype(F32)).astype(BF16)
     pl.semaphore_wait(barrier, len(greeted))
 
     numbers = itertools.count()
@@ -270,10 +273,8 @@
     left_top = send(cot.at[top], full_cot.at[tp, top], to_left)
     own = [fetch(weight.at[:, pl.ds(i * 1024, 1024)], full_weight.at[dp * 2 + i]) for i in range(2)]
 
-    key_copy.wait()
-    value_copy.wait()
-    mixed[...] = (key[...].astype(F32) * value[...].astype(F32)).astype(BF16)
-    mixed_sent = send(mixed.at[bottom], mixed_halo, to_next)
+    wide = [pl.ds(h * 2 * TILE, 2 * TILE) for h in range(2)]
+    mixed_sent = [send(mixed.at[bottom, cols], mixed_halo.at[:, cols], to_next) for cols in wide]
 
     def turn(owner, start, size):
         tokens, far_tokens = pl.ds(start, size), pl.ds(ROWS + start, size)
@@ -369,13 +370,12 @@
 
     for copy in state_copies:
         copy.wait()
-    mixed_sent.wait_recv()
-
-    share_import(0)
-    convolve(0)
-    share_import(1)
-    convolve(2)
-    gated_sent = send(gated.at[pl.ds(0, ROWS)], gated.at[pl.ds(ROWS, ROWS)], to_core)
+    gated_sent = []
+    for h in range(2):
+        mixed_sent[h].wait_recv()
+        convolve(2 * h)
+        half = gated.at[pl.ds(0, ROWS), wide[h]]
+        gated_sent.append(send(half, gated.at[pl.ds(ROWS, ROWS), wide[h]], to_core))
 
     first = [
         [gather(landing[quarter * PER_QUARTER + stream]) for stream in range(STREAMS)]
@@ -396,17 +396,17 @@
 
     first_targets = [to_near, to_far, to_side[0], to_side[1]]
 
-    def products(chunk, owner):
+    def products(owner, start=0, stop=4):
         low, group = lax.div(owner, 2), pl.ds(lax.rem(owner, 2) * 4, 4)
 
-        @pl.loop(0, 4)
+        @pl.loop(start, stop)
         def _(quarter):
             rows = turned[pl.ds(owner * 4, 4)].reshape(512, 2 * ROWS)
             block = matmul(rows, gated[:, columns(quarter)]).astype(BF16)
             partial[quarter, low, group] = block.reshape(4, 2, 64, TILE)
 
-    def halve(chunk, owner, stream):
-        for quarter in range(4):
+    def halve(chunk, owner, stream, quarters=(0, 1, 2, 3)):
+        for quarter in quarters:
             for i, slot in enumerate(first_slots(quarter, owner, y, z, False)):
                 send(
                     first_view(quarter, slot, stream),
@@ -415,29 +415,36 @@
                     first[quarter][stream],
                 )
 
+    share_import(0)
+    share_import(1)
+    turned_own.wait_recv()
+    gated_sent[0].wait_recv()
+    products(tp, 0, 2)
+    halve(0, tp, 0, (0, 1))
+    halve(0, tp, 1, (1,))
     share_import(2)
+    gated_sent[1].wait_recv()
+    products(tp, 2, 4)
+    for stream in range(STREAMS):
+        halve(0, tp, stream, (2, 3))
     right_top.wait_recv()
     forward_right = pass_cot(left, top, to_right)
     left_bottom.wait_recv()
     forward_left = pass_cot(right, bottom, to_left)
+    share_import(3)
+    share_near(0)
     turned_left = [turn(left, 0, 128)]
     turned_right = [turn(right, 128, 128)]
-    share_import(3)
-    share_near(0)
-    turned_own.wait_recv()
-    gated_sent.wait_recv()
-    products(0, tp)
-    halve(0, tp, 0)
     share_import(4)
-    share_near(1)
     share_import(5)
-    share_near(2)
     share_import(6)
-    share_near(3)
     right_bottom.wait_recv()
     turned_left.append(turn(left, 128, 128))
     left_top.wait_recv()
     turned_right.append(turn(right, 0, 128))
+    share_import(7)
+    share_near(1)
+    share_near(2)
     for copy in own:
         copy.wait()
     late = jnp.where(lax.div(across, 2) == dp, across, dp * 4 + 1 - tp)
@@ -448,23 +455,23 @@
         cols = columns(tile)
         grad_gated[:, cols] = matmul_nt(full_cot[early], full_weight[early, cols])
 
-    share_import(7)
-    share_near(4)
+    share_near(3)
     for copy in turned_left:
         copy.wait_recv()
-    products(1, left)
+    products(left)
     halve(1, left, 0)
+    share_near(4)
     share_near(5)
-    share_near(6)
     for copy in turned_right:
         copy.wait_recv()
-    products(2, right)
+    products(right)
     halve(2, right, 0)
     forward_right.wait_recv()
     forward_left.wait_recv()
     turned_across = turn(across, 0, ROWS)
+    share_near(6)
     share_near(7)
-    halve(0, tp, 1)
+    halve(0, tp, 1, (0,))
     halve(1, left, 1)
     @pl.loop(0, CHANNELS // TILE)
     def _(tile):
@@ -472,7 +479,7 @@
         grad_gated[:, cols] += matmul_nt(full_cot[late], full_weight[late, cols])
 
     turned_across.wait_recv()
-    products(3, across)
+    products(across)
     halve(3, across, 0)
     halve(2, right, 1)
     halve(3, across, 1)

time: 68.5 us -> 67.8 us (0.990)
  no operation moved by 1% of the time
where the time goes in v4:
time: 67.8 us; the launch traced here: 67.7 us
  Pallas kernels  67.1 us (99%)
    pallas_call x1, Pallas kernels, per_device(): pl.pallas_call(kernel, out_shape=[pltpu.VMEM((ROWS, CHANNELS), BF16), plt...  65.6 us
    pallas_call x1, Pallas kernels, per_device(): pl.pallas_call(hand_on, out_shape=[jax.ShapeDtypeStruct(x.shape, x.dtype)...  1.45 us

profile of v4, /device:TPU:1, one launch (start us, length us, event | category | flops | bytes accessed | tf_op | source)
XLA Modules:
  0.0 67.7 jit_solution(7937299643797156595)
XLA Ops:
  0.6 65.6 %shard_map.136 = (bf16[256,1024]{1,0:T(8,128)(2,1)S(1)}, bf16[256,1024]{1,0:T(8,128)(2,1)S(1)}, bf16[256,1024]{1,0:T(8,128)(2,1)S(1)}, f32[8,8,16,128]{3,2,1,0:T...) custom-call(bf16[256,1024]{1,0:T(8,128)(2,1)} %bitcast.15, bf16[256,1024]{1,0:T(8,128)(2,1)} %bitcast.16, ...), custom_call_target="tpu_custom_call" | custom-call | tf_op jit(solution)/shard_map/pallas_call | solution.py:683
  66.3 1.5 %shard_map.137 = (bf16[1,256,1024]{2,1,0:T(8,128)(2,1)}, bf16[1,256,1024]{2,1,0:T(8,128)(2,1)}, bf16[1,256,1024]{2,1,0:T(8,128)(2,1)}, f32[1024,128]{1,0:T(8,128)}, f32[1024]{0:T(1024)}, /*index=5*/f32[64,1024]{1,0:T(8,128)}) custom-call(bf16[1,256,1024]{2,1,0:T(8,128)(2,1)S(1)} %bitcast.10, bf16[1,256,1024]{2,1,0:T(8,128)(2,1)S(1)} %bitcast.11, ...), custom_call_target="tpu_custom_call" | custom-call | tf_op jit(solution)/shard_map/pallas_call | solution.py:718

commit v5 on v4

--- a/solution.py
+++ b/solution.py
@@ -490,6 +490,7 @@
     from_corner[0][0].wait_recv()
     share_core("corner", 0)
     signal_sent = gather(signal_halo)
+    near_sums = gather(near_land)
 
     def finish(tile, kind):
         from_core[kind][0].wait_recv()
@@ -512,7 +513,16 @@
         )
         for i in range(TILE // 128):
             block = lags[:, i * 128 : (i + 1) * 128].T
-            lag_sum[tile * (TILE // 128) + i] = block.astype(BF16)
+            owner = tile * 2 + i
+            ahead_by = lax.rem(owner + 8 - member, 8)
+            lag_sum[owner] = block.astype(BF16)
+
+            @pl.when(ahead_by > 0)
+            def _():
+                send(
+                    lag_sum.at[owner], near_land.at[ahead_by - 1], to_member(owner), near_sums, 0
+                )
+
 
     rounds = {}
 
@@ -575,17 +585,14 @@
 
     finish(y[0] * 2 + odd, "here")
     finish((1 - y[0]) * 2 + odd, "beside")
+    combine_all(0, 0)
     from_corner[1][0].wait_recv()
     share_core("corner", 1)
     finish(y[0] * 2 + 1 - odd, "above")
     finish((1 - y[0]) * 2 + 1 - odd, "corner")
 
-    near_sums = gather(near_land)
-    for i in range(1, 8):
-        send(lag_sum.at[members[i]], near_land.at[i - 1], to_member(members[i]), near_sums, 0)
-
-    combine_all(0, 0)
     combine_all(0, 1)
+    combine_all(1, 0)
     near_sums[0].wait_recv()
     total = lag_sum[member].astype(F32)
     for i in range(7):
@@ -595,7 +602,6 @@
     for i in range(1, 8):
         send(lag_mid.at[heights[i]], far_land.at[i - 1], place(y, heights[i], core), far_sums, 1)
 
-    combine_all(1, 0)
     signal_sent[0].wait_recv()
 
     restore_back(0)

time: 67.8 us -> 67 us (0.988)
  Pallas kernels: 67.1 us -> 66.3 us
    pallas_call x1, Pallas kernels: 65.6 us -> 64.8 us  [per_device(): pl.pallas_call(kernel, out_shape=[pltpu.VMEM((ROWS, CHANNELS), BF16), plt...]
where the time goes in v5:
time: 67 us; the launch traced here: 66.9 us
  Pallas kernels  66.3 us (99%)
    pallas_call x1, Pallas kernels, per_device(): pl.pallas_call(kernel, out_shape=[pltpu.VMEM((ROWS, CHANNELS), BF16), plt...  64.8 us
    pallas_call x1, Pallas kernels, per_device(): pl.pallas_call(hand_on, out_shape=[jax.ShapeDtypeStruct(x.shape, x.dtype)...  1.45 us

profile of v5, /device:TPU:1, one launch (start us, length us, event | category | flops | bytes accessed | tf_op | source)
XLA Modules:
  0.0 66.9 jit_solution(1285461859699948611)
XLA Ops:
  0.6 64.8 %shard_map.136 = (bf16[256,1024]{1,0:T(8,128)(2,1)S(1)}, bf16[256,1024]{1,0:T(8,128)(2,1)S(1)}, bf16[256,1024]{1,0:T(8,128)(2,1)S(1)}, f32[8,8,16,128]{3,2,1,0:T...) custom-call(bf16[256,1024]{1,0:T(8,128)(2,1)} %bitcast.15, bf16[256,1024]{1,0:T(8,128)(2,1)} %bitcast.16, ...), custom_call_target="tpu_custom_call" | custom-call | tf_op jit(solution)/shard_map/pallas_call | solution.py:689
  65.4 1.5 %shard_map.137 = (bf16[1,256,1024]{2,1,0:T(8,128)(2,1)}, bf16[1,256,1024]{2,1,0:T(8,128)(2,1)}, bf16[1,256,1024]{2,1,0:T(8,128)(2,1)}, f32[1024,128]{1,0:T(8,128)}, f32[1024]{0:T(1024)}, /*index=5*/f32[64,1024]{1,0:T(8,128)}) custom-call(bf16[1,256,1024]{2,1,0:T(8,128)(2,1)S(1)} %bitcast.10, bf16[1,256,1024]{2,1,0:T(8,128)(2,1)S(1)} %bitcast.11, ...), custom_call_target="tpu_custom_call" | custom-call | tf_op jit(solution)/shard_map/pallas_call | solution.py:724

commit v6 on v5

--- a/solution.py
+++ b/solution.py
@@ -606,7 +606,6 @@
 
     restore_back(0)
     combine_all(1, 1)
-    combine_all(2, 0)
     far_sums[0].wait_recv()
     total = lag_mid[z]
     for i in range(7):
@@ -614,13 +613,14 @@
     lag_out[member, z] = (total * scale).astype(BF16)
     mine = lag_out.at[member, z]
     copies = [send(mine, mine, place(y, heights[i], core), None, 2) for i in range(1, 8)]
+    combine_all(2, 0)
     restore_back(2)
     combine_all(2, 1)
-    combine_all(3, 0)
     for copy in copies:
         copy.wait_recv()
     mine = lag_out.at[member]
     copies = [send(mine, mine, to_member(members[i]), None, 3) for i in range(1, 8)]
+    combine_all(3, 0)
     combine_all(3, 1)
     combine_all(4, 0)
     for copy in copies:

time: 67 us -> 66.8 us (level)
  no operation moved by 1% of the time
where the time goes in v6:
time: 66.8 us; the launch traced here: 66.5 us
  Pallas kernels  65.9 us (99%)
    pallas_call x1, Pallas kernels, per_device(): pl.pallas_call(kernel, out_shape=[pltpu.VMEM((ROWS, CHANNELS), BF16), plt...  64.4 us
    pallas_call x1, Pallas kernels, per_device(): pl.pallas_call(hand_on, out_shape=[jax.ShapeDtypeStruct(x.shape, x.dtype)...  1.45 us

profile of v6, /device:TPU:1, one launch (start us, length us, event | category | flops | bytes accessed | tf_op | source)
XLA Modules:
  0.0 66.5 jit_solution(15093305550792744424)
XLA Ops:
  0.6 64.4 %shard_map.136 = (bf16[256,1024]{1,0:T(8,128)(2,1)S(1)}, bf16[256,1024]{1,0:T(8,128)(2,1)S(1)}, bf16[256,1024]{1,0:T(8,128)(2,1)S(1)}, f32[8,8,16,128]{3,2,1,0:T...) custom-call(bf16[256,1024]{1,0:T(8,128)(2,1)} %bitcast.15, bf16[256,1024]{1,0:T(8,128)(2,1)} %bitcast.16, ...), custom_call_target="tpu_custom_call" | custom-call | tf_op jit(solution)/shard_map/pallas_call | solution.py:689
  65.0 1.5 %shard_map.137 = (bf16[1,256,1024]{2,1,0:T(8,128)(2,1)}, bf16[1,256,1024]{2,1,0:T(8,128)(2,1)}, bf16[1,256,1024]{2,1,0:T(8,128)(2,1)}, f32[1024,128]{1,0:T(8,128)}, f32[1024]{0:T(1024)}, /*index=5*/f32[64,1024]{1,0:T(8,128)}) custom-call(bf16[1,256,1024]{2,1,0:T(8,128)(2,1)S(1)} %bitcast.10, bf16[1,256,1024]{2,1,0:T(8,128)(2,1)S(1)} %bitcast.11, ...), custom_call_target="tpu_custom_call" | custom-call | tf_op jit(solution)/shard_map/pallas_call | solution.py:724
